TPU v7x, 128 devices: a whole 4x4x4 slice. The times are simulated.
128 devices in a mesh: gx: 16 (over y, x_hi, core), gy: 8 (over x_lo, z).
Axes of the slice: x: 4 (x_hi: 2, x_lo: 2; x = x_hi * 2 + x_lo), y: 4, z: 4, core: 2. Of those that a mesh axis runs over, the one named last changes fastest.
Arguments:
- ocean_depth: float32 [4096, 4096], P('gx', 'gy'), may hold values from 0.5 to 8
- wet_mask: int32 [4096, 4096], P('gx', 'gy'), may hold values 0 or 1
- manning: float32 [4096, 4096], P('gx', 'gy'), may hold values from 0.5 to 5
- fault_slip: float32 [2048], P(('gx', 'gy')), may hold values from 0.3 to 1.2
- pattern: float32 [32768, 8, 128], P(('gx', 'gy')), may hold values from -1 to 1
- foot_tile: int32 [32768, 1], P(('gx', 'gy')), may hold values from 0 to 127; in each aligned block of 256 rows (0 to 255, 256 to 511, ...) at most 4 rows name the same one
- foot_block: int32 [32768], P(('gx', 'gy')), may hold values from 0 to 127
- gauge_row: int32 [2048], replicated, may hold values from 0 to 4095, as said below
- gauge_col: int32 [2048], replicated, may hold values from 0 to 4095, as said below
- observed: float32 [4, 2048], replicated, may hold values from -6 to 6
Outputs:
- final_eta: float32 [4096, 4096], P('gx', 'gy')
- readings: float32 [4, 2048], replicated
- source_adjoint: float32 [4096, 4096], P('gx', 'gy')
- grad_slip: float32 [2048], P(('gx', 'gy'))
Inputs may be any that keep to these rules, and one draw needn't show every extreme that they name: `foot_tile`: the 256 rows of one device name no tile more than 4 times, a bound that some block reaches. Tile t is the one at tile row t // 8 and tile column t % 8. `gauge_row`: gauges 16 * t to 16 * t + 15 lie in tile t, within three cells of one of its edges. `gauge_col`: see gauge_row.
All inputs are finite; a program needn't handle non-finite values. No bound on the sum of `wet_mask` on one device may be relied on, other than what follows from the above.
Results may differ from a plain program's by a relative error of at most 0.0003.
Values sent between devices are 32-bit elements; how exact they have to be, the bound alone decides.
No kernel may reach another device: no remote copies, remote signals or barrier semaphores. Data moves between devices by JAX's collectives and lax.ppermute only.
A program may use at most 128 MiB of HBM per device.

v0:
```python
from functools import partial

import jax
import jax.numpy as jnp
from jax import lax
from jax.sharding import PartitionSpec as P

wave_gain = 0.2
mass_gain = 0.2
min_depth = 0.25
speed_floor = 0.01


def shifted(shard, axis, by):
    devices = lax.axis_size(axis)
    pairs = [(i, i + by) for i in range(devices) if 0 <= i + by < devices]
    return lax.ppermute(shard, axis, pairs)


def eastward(field, column):
    return jnp.concatenate([field[:, 1:], column[:, None]], axis=1)


def southward(field, row_edge):
    return jnp.concatenate([field[1:], row_edge[None]], axis=0)


def face_flux(
    flux, here, there, depth_here, depth_there, wet_here, wet_there, fric_here, fric_there
):
    total_depth = jnp.maximum(0.5 * (depth_here + here + depth_there + there), min_depth)
    pushed = flux - wave_gain * total_depth * (there - here)
    roughness = 0.5 * (fric_here + fric_there)
    drag_factor = 1.0 + roughness * jnp.sqrt(pushed * pushed + speed_floor) / jnp.power(
        total_depth, 7.0 / 3.0
    )
    return wet_here * wet_there * pushed / drag_factor


def fluxes(statics, static_east, static_south, surface, east_rim, south_rim, flux_east, flux_south):
    depth_here, wet_here, fric_here = (statics[0], statics[1], statics[2])
    next_east = face_flux(
        flux_east,
        surface,
        eastward(surface, east_rim),
        depth_here,
        eastward(depth_here, static_east[0]),
        wet_here,
        eastward(wet_here, static_east[1]),
        fric_here,
        eastward(fric_here, static_east[2]),
    )
    next_south = face_flux(
        flux_south,
        surface,
        southward(surface, south_rim),
        depth_here,
        southward(depth_here, static_south[0]),
        wet_here,
        southward(wet_here, static_south[1]),
        fric_here,
        southward(fric_here, static_south[2]),
    )
    return (next_east, next_south)


def surface_step(wet_cells, surface, next_east, next_south, west_rim, north_rim):
    left_flux = jnp.concatenate([west_rim[:, None], next_east[:, :-1]], axis=1)
    upper_flux = jnp.concatenate([north_rim[None], next_south[:-1]], axis=0)
    return wet_cells * (surface - mass_gain * (next_east - left_flux + next_south - upper_flux))


def tile_from_blocks(blocks, rows_here, cols_here):
    return (
        blocks.reshape(rows_here // 8, cols_here // 128, 8, 128)
        .transpose(0, 2, 1, 3)
        .reshape(rows_here, cols_here)
    )


def blocks_from_tile(field):
    rows_here, cols_here = field.shape
    return (
        field.reshape(rows_here // 8, 8, cols_here // 128, 128)
        .transpose(0, 2, 1, 3)
        .reshape(-1, 1024)
    )


def body(
    ocean_depth,
    wet_mask,
    manning,
    fault_slip,
    pattern,
    foot_tile,
    foot_block,
    gauge_row,
    gauge_col,
    observed,
):
    rows_here, cols_here = ocean_depth.shape
    step_count = observed.shape[0]
    wet_cells = wet_mask.astype(jnp.float32)
    width_x = lax.axis_size("gx")
    width_y = lax.axis_size("gy")
    devices = width_x * width_y
    entries = pattern.shape[0]
    per_fault = entries // fault_slip.shape[0]
    capacity = max(2, (2 * entries + devices - 1) // devices)
    target = foot_tile[:, 0]
    row_order = jnp.arange(entries, dtype=jnp.int32)
    earlier = (target[:, None] == target[None, :]) & (row_order[:, None] > row_order[None, :])
    slot_rank = jnp.sum(earlier.astype(jnp.int32), axis=1)
    slot_place = target * capacity + slot_rank
    weights = jnp.repeat(fault_slip, per_fault)
    out_pattern = (
        jnp.zeros((devices * capacity, 1024), jnp.float32)
        .at[slot_place]
        .set(pattern.reshape(entries, 1024))
    )
    out_slip = jnp.zeros((devices * capacity,), jnp.float32).at[slot_place].set(weights)
    out_block = (
        jnp.zeros((devices * capacity,), jnp.float32)
        .at[slot_place]
        .set(foot_block.astype(jnp.float32))
    )
    in_pattern, in_slip, in_block = (
        lax.all_to_all(out_pattern, ("gx", "gy"), split_axis=0, concat_axis=0, tiled=True),
        lax.all_to_all(out_slip, ("gx", "gy"), split_axis=0, concat_axis=0, tiled=True),
        lax.all_to_all(out_block, ("gx", "gy"), split_axis=0, concat_axis=0, tiled=True),
    )
    block_index = in_block.astype(jnp.int32)
    start_blocks = (
        jnp.zeros((rows_here * cols_here // 1024, 1024), jnp.float32)
        .at[block_index]
        .add(in_slip[:, None] * in_pattern)
    )
    surface = tile_from_blocks(start_blocks, rows_here, cols_here) * wet_cells
    local_row = gauge_row - lax.axis_index("gx") * rows_here
    local_col = gauge_col - lax.axis_index("gy") * cols_here
    owned = (local_row >= 0) & (local_row < rows_here) & (local_col >= 0) & (local_col < cols_here)
    safe_row = jnp.where(owned, local_row, 0)
    safe_col = jnp.where(owned, local_col, 0)
    owned_weight = owned.astype(jnp.float32)
    statics = jnp.stack([ocean_depth, wet_cells, manning])
    static_east = shifted(statics[:, :, 0], "gy", -1)
    static_south = shifted(statics[:, 0, :], "gx", -1)
    advance_flux = partial(fluxes, statics, static_east, static_south)
    advance_surface = partial(surface_step, wet_cells)
    flux_east = jnp.zeros_like(surface)
    flux_south = jnp.zeros_like(surface)
    saved = []
    gathered = []
    for step_index in range(step_count):
        east_rim = shifted(surface[:, 0], "gy", -1)
        south_rim = shifted(surface[0, :], "gx", -1)
        next_east, next_south = advance_flux(surface, east_rim, south_rim, flux_east, flux_south)
        west_rim = shifted(next_east[:, -1], "gy", 1)
        north_rim = shifted(next_south[-1, :], "gx", 1)
        saved.append(
            (
                surface,
                east_rim,
                south_rim,
                flux_east,
                flux_south,
                next_east,
                next_south,
                west_rim,
                north_rim,
            )
        )
        surface = advance_surface(surface, next_east, next_south, west_rim, north_rim)
        flux_east, flux_south = (next_east, next_south)
        gathered.append(surface[safe_row, safe_col] * owned_weight)
    readings = jnp.stack([lax.psum(local_read, ("gx", "gy")) for local_read in gathered])
    misfit_terms = readings - observed
    cot_surface = jnp.zeros_like(surface)
    cot_east = jnp.zeros_like(surface)
    cot_south = jnp.zeros_like(surface)
    for step_index in reversed(range(step_count)):
        (
            old_surface,
            east_rim,
            south_rim,
            old_east,
            old_south,
            next_east,
            next_south,
            west_rim,
            north_rim,
        ) = saved[step_index]
        gauge_seed = (
            jnp.zeros_like(surface)
            .at[safe_row, safe_col]
            .add(misfit_terms[step_index] * owned_weight)
        )
        cot_surface = cot_surface + gauge_seed
        unused, surface_fn = jax.vjp(
            advance_surface, old_surface, next_east, next_south, west_rim, north_rim
        )
        part_surface, part_east, part_south, cot_west, cot_north = surface_fn(cot_surface)
        part_east = part_east + cot_east
        part_south = part_south + cot_south
        part_east = part_east.at[:, -1].add(shifted(cot_west, "gy", -1))
        part_south = part_south.at[-1, :].add(shifted(cot_north, "gx", -1))
        unused_pair, flux_fn = jax.vjp(
            advance_flux, old_surface, east_rim, south_rim, old_east, old_south
        )
        flux_surface, cot_east_rim, cot_south_rim, cot_east, cot_south = flux_fn(
            (part_east, part_south)
        )
        cot_surface = part_surface + flux_surface
        cot_surface = cot_surface.at[:, 0].add(shifted(cot_east_rim, "gy", 1))
        cot_surface = cot_surface.at[0, :].add(shifted(cot_south_rim, "gx", 1))
    cot_blocks = blocks_from_tile(cot_surface * wet_cells)
    per_slot = jnp.sum(cot_blocks[block_index] * in_pattern, axis=1)
    returned = lax.all_to_all(per_slot, ("gx", "gy"), split_axis=0, concat_axis=0, tiled=True)
    grad_slip = jnp.sum(returned[slot_place].reshape(-1, per_fault), axis=1)
    return (surface, readings, cot_surface, grad_slip)


def solution(mesh):
    placed = (
        P("gx", "gy"),
        P("gx", "gy"),
        P("gx", "gy"),
        P(("gx", "gy")),
        P(("gx", "gy"), None, None),
        P(("gx", "gy"), None),
        P(("gx", "gy")),
        P(),
        P(),
        P(),
    )
    return jax.shard_map(
        body,
        mesh=mesh,
        in_specs=placed,
        out_specs=(P("gx", "gy"), P(), P("gx", "gy"), P(("gx", "gy"))),
        check_vma=False,
    )
```

profile of v0, /device:TPU:1, one launch (start us, length us, event | category | flops | bytes accessed | tf_op | source)
XLA Modules:
  0.0 592.0 jit_solution(286648592002307185)
XLA Ops:
  5.1 11.5 %all-to-all-start = ((f32[128,4,1]{1,2,0:T(1,128)}), f32[128,4,1]{1,2,0:T(1,128)S(1)}, u32[]{:S(2)}, u32[]{:S(2)}) async-start(f32[128,4,1]{1,2,0:T(1,128)} %bitcast.3), calls=%async_computation | async-start | bytes 131072 | tf_op jit(solution)/shard_map/all_to_all | solution.py:131
  19.5 6.9 %all-to-all-done = f32[128,4,1]{1,2,0:T(1,128)S(1)} async-done(((f32[128,4,1]{1,2,0:T(1,128)}), f32[128,4,1]{1,2,0:T(1,128)S(1)}, u32[]{:S(2)}, u32[]{:S(2)}) %all-to-all-start) | async-done | bytes 2080 | tf_op jit(solution)/shard_map/all_to_all | solution.py:131
  35.1 5.3 all-to-all-done.1
  40.4 4.5 all-to-all-start.2
  64.9 9.5 %all-to-all-done.2 = f32[128,4,1024]{2,1,0:T(4,128)S(1)} async-done(((f32[128,4,1024]{2,1,0:T(4,128)}), f32[128,4,1024]{2,1,0:T(4,128)S(1)}, u32[]{:S(2)}, u32[]{:S(2)}) %all-to-all-start.2) | async-done | bytes 2097184 | tf_op jit(solution)/shard_map/all_to_all | solution.py:129
  76.4 6.7 %scatter_custom_fusion.3 = f32[128,1024]{1,0:T(8,128)} fusion(s32[512]{0:T(512)} %bitcast.166, f32[512,1024]{1,0:T(8,128)} %all_to_all.34, f32[512]{0:T(512)S(1)} %copy-done.77, f32[]{:T(128)} %constant.399.clone.1), kind=kCustom, calls=%fused_computation.15 | custom fusion | flops 1048576 | bytes 2624000 | tf_op jit(solution)/shard_map/scatter-add | solution.py:137
  118.8 4.8 fusion.72
  143.6 5.0 fusion.70
  153.8 5.2 collective-permute-start.13
  172.2 5.2 fusion.68
  178.4 5.9 collective-permute-start.15
  184.3 5.4 collective-permute-start.17
  190.4 25.4 %gather_fusion = f32[2048]{0:T(1024)} fusion(f32[256,512]{1,0:T(8,128)S(1)} %fusion.14, s32[2048]{0:T(1024)S(1)} %bitcast.118), kind=kCustom, calls=%fused_computation | custom fusion | bytes 32768 | tf_op jit(solution)/shard_map/gather | solution.py:176
  215.8 25.4 %gather_fusion.1 = f32[2048]{0:T(1024)} fusion(f32[256,512]{1,0:T(8,128)S(1)} %fusion.20, s32[2048]{0:T(1024)S(1)} %bitcast.119), kind=kCustom, calls=%fused_computation.1 | custom fusion | bytes 32768 | tf_op jit(solution)/shard_map/gather | solution.py:176
  241.2 25.4 %gather_fusion.2 = f32[2048]{0:T(1024)} fusion(f32[256,512]{1,0:T(8,128)S(1)} %fusion.25, s32[2048]{0:T(1024)S(1)} %bitcast.120), kind=kCustom, calls=%fused_computation.2 | custom fusion | bytes 32768 | tf_op jit(solution)/shard_map/gather | solution.py:176
  269.3 16.6 %gather_fusion.3 = f32[2048]{0:T(1024)S(1)} fusion(f32[256,512]{1,0:T(8,128)S(1)} %fusion.30, s32[2048]{0:T(1024)S(1)} %bitcast.121), kind=kCustom, calls=%fused_computation.3 | custom fusion | bytes 32768 | tf_op jit(solution)/shard_map/gather | solution.py:176
  286.0 71.3 %all-reduce.16 = (f32[1,2048]{1,0:T(1,128)S(1)}, f32[1,2048]{1,0:T(1,128)S(1)}, f32[1,2048]{1,0:T(1,128)S(1)}, f32[1,2048]{1,0:T(1,128)S(1)}) all-reduce(f32[1,2048]{1,0:T(1,128)S(1)} %bitcast.156, f32[1,2048]{1,0:T(1,128)S(1)} %bitcast.157, f32[1,2048]{1,0:T(1,128)S(1)} %bitcast.158, ...), channel_id=1, replica_groups=mesh['gx'=16,'gy'=8] {'gx','gy'}, use_global_device_ids=true, to_apply=%region_8.9 | all-reduce | flops 8192 | bytes 65536 | tf_op jit(solution)/shard_map/psum | solution.py:177
  358.7 14.8 %scatter_custom_fusion.4 = f32[131072]{0:T(1024)S(1)} fusion(s32[2048]{0:T(1024)S(1)} %broadcast_select_fusion, f32[2048]{0:T(1024)S(1)} %get-tuple-element.312, f32[]{:T(128)} %constant.399.clone.1), kind=kCustom, calls=%fused_computation.175 | custom fusion | flops 2048 | bytes 524292
  392.0 5.2 fusion.59
  400.4 4.9 collective-permute-start.21
  411.4 15.1 %scatter_fusion = f32[131072]{0:T(1024)S(1)} fusion(f32[131072]{0:T(1024)S(1)} %bitcast.124, s32[2048]{0:T(1024)S(1)} %broadcast_select_fusion, f32[2048]{0:T(1024)} %get-tuple-element.311), kind=kCustom, calls=%fused_computation.11 | custom fusion | flops 2048 | bytes 32768
  441.4 4.9 fusion.61
  446.5 4.4 collective-permute-start.24
  451.5 6.3 %collective-permute-start.25 = (f32[512]{0:T(512)}, f32[512]{0:T(512)}, u32[]{:S(2)}, u32[]{:S(2)}) collective-permute-start(f32[512]{0:T(512)} %bitcast.56), channel_id=1, source_target_pairs={{0,8},{8,16},{16,24},{24,32},{32,40},{40,48},{48,56},{56,64},{64,7... | collective-permute-start | bytes 6152 | tf_op jit(solution)/shard_map/ppermute | solution.py:17
  462.4 14.9 %scatter_fusion.1 = f32[131072]{0:T(1024)S(1)} fusion(f32[131072]{0:T(1024)S(1)} %bitcast.125, s32[2048]{0:T(1024)S(1)} %broadcast_select_fusion, f32[2048]{0:T(1024)S(1)} %get-tuple-element.310), kind=kCustom, calls=%fused_computation.12 | custom fusion | flops 2048 | bytes 32768
  492.6 4.8 fusion.63
  501.5 6.3 %collective-permute-start.29 = (f32[512]{0:T(512)S(1)}, f32[512]{0:T(512)S(1)}, u32[]{:S(2)}, u32[]{:S(2)}) collective-permute-start(f32[512]{0:T(512)S(1)} %bitcast.185), channel_id=1, source_target_pairs={{0,8},{8,16},{16,24},{24,32},{32,40},{40,48},{48,56},{56,64},{64,7... | collective-permute-start | bytes 6152 | tf_op jit(solution)/shard_map/ppermute | solution.py:17
  511.7 14.9 %scatter_fusion.2 = f32[131072]{0:T(1024)S(1)} fusion(f32[131072]{0:T(1024)S(1)} %bitcast.123, s32[2048]{0:T(1024)S(1)} %broadcast_select_fusion, f32[2048]{0:T(1024)S(1)} %copy-done.65), kind=kCustom, calls=%fused_computation.13 | custom fusion | flops 2048 | bytes 32768
  540.6 4.5 fusion.57
  549.0 6.3 %collective-permute-start.33 = (f32[512]{0:T(512)S(1)}, f32[512]{0:T(512)S(1)}, u32[]{:S(2)}, u32[]{:S(2)}) collective-permute-start(f32[512]{0:T(512)S(1)} %bitcast.184), channel_id=1, source_target_pairs={{0,8},{8,16},{16,24},{24,32},{32,40},{40,48},{48,56},{56,64},{64,7... | collective-permute-start | bytes 6152 | tf_op jit(solution)/shard_map/ppermute | solution.py:17
  565.9 12.4 %all-to-all-start.3 = ((f32[128,4,1]{1,2,0:T(1,128)}), f32[128,4,1]{1,2,0:T(1,128)S(1)}, u32[]{:S(2)}, u32[]{:S(2)}) async-start(f32[128,4,1]{1,2,0:T(1,128)} %bitcast.74), calls=%async_computation.3 | async-start | bytes 131072 | tf_op jit(solution)/shard_map/all_to_all | solution.py:219
  578.3 9.8 %all-to-all-done.3 = f32[128,4,1]{1,2,0:T(1,128)S(1)} async-done(((f32[128,4,1]{1,2,0:T(1,128)}), f32[128,4,1]{1,2,0:T(1,128)S(1)}, u32[]{:S(2)}, u32[]{:S(2)}) %all-to-all-start.3) | async-done | bytes 2080 | tf_op jit(solution)/shard_map/all_to_all | solution.py:219
  (423 shorter events, 219.9 us)
Async XLA Ops:
  5.1 21.3 %all-to-all-start = ((f32[128,4,1]{1,2,0:T(1,128)}), f32[128,4,1]{1,2,0:T(1,128)S(1)}, u32[]{:S(2)}, u32[]{:S(2)}) async-start(f32[128,4,1]{1,2,0:T(1,128)} %bitcast.3), calls=%async_computation | async-start | bytes 131072 | tf_op jit(solution)/shard_map/all_to_all | solution.py:131
  26.4 14.0 %all-to-all-start.1 = ((f32[128,4,1]{1,2,0:T(1,128)}), f32[128,4,1]{1,2,0:T(1,128)S(1)}, u32[]{:S(2)}, u32[]{:S(2)}) async-start(f32[128,4,1]{1,2,0:T(1,128)} %bitcast.5), calls=%async_computation.1 | async-start | bytes 131072 | tf_op jit(solution)/shard_map/all_to_all | solution.py:130
  40.4 34.0 %all-to-all-start.2 = ((f32[128,4,1024]{2,1,0:T(4,128)}), f32[128,4,1024]{2,1,0:T(4,128)S(1)}, u32[]{:S(2)}, u32[]{:S(2)}) async-start(f32[128,4,1024]{2,1,0:T(4,128)} %all_to_all.32), calls=%async_computation.2 | async-start | bytes 4194304 | tf_op jit(solution)/shard_map/all_to_all | solution.py:129
  48.0 37.8 %collective-permute-start.3 = (f32[3,512]{1,0:T(4,128)S(1)}, f32[3,512]{1,0:T(4,128)}, u32[]{:S(2)}, u32[]{:S(2)}) collective-permute-start(f32[3,512]{1,0:T(4,128)S(1)} %fusion.75), channel_id=1, source_target_pairs={{8,0},{16,8},{24,16},{32,24},{40,32},{48,40},{56,48},{64,56},{72,6... | collective-permute-start | bytes 18440 | tf_op jit(solution)/shard_map/ppermute | solution.py:17
  53.3 11.2 %collective-permute-start = (f32[3,256]{1,0:T(4,128)S(1)}, f32[3,256]{1,0:T(4,128)S(1)}, u32[]{:S(2)}, u32[]{:S(2)}) collective-permute-start(f32[3,256]{1,0:T(4,128)S(1)} %bitcast.168), channel_id=1, source_target_pairs={{1,0},{2,1},{3,2},{4,3},{5,4},{6,5},{7,6},{9,8},{10,9},{11,10},{12... | collective-permute-start | bytes 9224 | tf_op jit(solution)/shard_map/ppermute | solution.py:17
  84.4 8.3 %collective-permute-start.1 = (f32[256]{0:T(256)S(1)}, f32[256]{0:T(256)S(1)}, u32[]{:S(2)}, u32[]{:S(2)}) collective-permute-start(f32[256]{0:T(256)S(1)} %slice_reduce_fusion.15), channel_id=1, source_target_pairs={{1,0},{2,1},{3,2},{4,3},{5,4},{6,5},{7,6},{9,8},{10,9},{11,10},{12... | collective-permute-start | bytes 3080 | tf_op jit(solution)/shard_map/ppermute | solution.py:17
  89.0 12.6 %collective-permute-start.4 = (f32[512]{0:T(512)}, f32[512]{0:T(512)S(1)}, u32[]{:S(2)}, u32[]{:S(2)}) collective-permute-start(f32[512]{0:T(512)} %bitcast.15), channel_id=1, source_target_pairs={{8,0},{16,8},{24,16},{32,24},{40,32},{48,40},{56,48},{64,56},{72,6... | collective-permute-start | bytes 6152 | tf_op jit(solution)/shard_map/ppermute | solution.py:17
  97.3 10.4 %collective-permute-start.2 = (f32[256]{0:T(256)S(1)}, f32[256]{0:T(256)S(1)}, u32[]{:S(2)}, u32[]{:S(2)}) collective-permute-start(f32[256]{0:T(256)S(1)} %slice_reduce_fusion.14), channel_id=1, source_target_pairs={{0,1},{1,2},{2,3},{3,4},{4,5},{5,6},{6,7},{8,9},{9,10},{10,11},{11... | collective-permute-start | bytes 3080 | tf_op jit(solution)/shard_map/ppermute | solution.py:17
  110.6 5.1 collective-permute-start.6
  111.9 7.0 %collective-permute-start.8 = (f32[512]{0:T(512)S(1)}, f32[512]{0:T(512)S(1)}, u32[]{:S(2)}, u32[]{:S(2)}) collective-permute-start(f32[512]{0:T(512)S(1)} %bitcast.186), channel_id=1, source_target_pairs={{8,0},{16,8},{24,16},{32,24},{40,32},{48,40},{56,48},{64,56},{72,6... | collective-permute-start | bytes 6152 | tf_op jit(solution)/shard_map/ppermute | solution.py:17
  123.8 7.6 %collective-permute-start.7 = (f32[256]{0:T(256)S(1)}, f32[256]{0:T(256)S(1)}, u32[]{:S(2)}, u32[]{:S(2)}) collective-permute-start(f32[256]{0:T(256)S(1)} %slice_reduce_fusion.12), channel_id=1, source_target_pairs={{0,1},{1,2},{2,3},{3,4},{4,5},{5,6},{6,7},{8,9},{9,10},{10,11},{11... | collective-permute-start | bytes 3080 | tf_op jit(solution)/shard_map/ppermute | solution.py:17
  135.0 6.5 %collective-permute-start.10 = (f32[256]{0:T(256)S(1)}, f32[256]{0:T(256)S(1)}, u32[]{:S(2)}, u32[]{:S(2)}) collective-permute-start(f32[256]{0:T(256)S(1)} %slice_reduce_fusion.11), channel_id=1, source_target_pairs={{1,0},{2,1},{3,2},{4,3},{5,4},{6,5},{7,6},{9,8},{10,9},{11,10},{12... | collective-permute-start | bytes 3080 | tf_op jit(solution)/shard_map/ppermute | solution.py:17
  136.3 7.3 %collective-permute-start.12 = (f32[512]{0:T(512)}, f32[512]{0:T(512)}, u32[]{:S(2)}, u32[]{:S(2)}) collective-permute-start(f32[512]{0:T(512)} %bitcast.27), channel_id=1, source_target_pairs={{8,0},{16,8},{24,16},{32,24},{40,32},{48,40},{56,48},{64,56},{72,6... | collective-permute-start | bytes 6152 | tf_op jit(solution)/shard_map/ppermute | solution.py:17
  149.5 10.2 %collective-permute-start.11 = (f32[256]{0:T(256)S(1)}, f32[256]{0:T(256)S(1)}, u32[]{:S(2)}, u32[]{:S(2)}) collective-permute-start(f32[256]{0:T(256)S(1)} %slice_reduce_fusion.10), channel_id=1, source_target_pairs={{0,1},{1,2},{2,3},{3,4},{4,5},{5,6},{6,7},{8,9},{9,10},{10,11},{11... | collective-permute-start | bytes 3080 | tf_op jit(solution)/shard_map/ppermute | solution.py:17
  153.8 6.8 %collective-permute-start.13 = (f32[512]{0:T(512)S(1)}, f32[512]{0:T(512)S(1)}, u32[]{:S(2)}, u32[]{:S(2)}) collective-permute-start(f32[512]{0:T(512)S(1)} %bitcast.189), channel_id=1, source_target_pairs={{0,8},{8,16},{16,24},{24,32},{32,40},{40,48},{48,56},{56,64},{64,7... | collective-permute-start | bytes 6152 | tf_op jit(solution)/shard_map/ppermute | solution.py:17
  163.8 6.4 %collective-permute-start.14 = (f32[256]{0:T(256)S(1)}, f32[256]{0:T(256)S(1)}, u32[]{:S(2)}, u32[]{:S(2)}) collective-permute-start(f32[256]{0:T(256)S(1)} %slice_reduce_fusion.9), channel_id=1, source_target_pairs={{1,0},{2,1},{3,2},{4,3},{5,4},{6,5},{7,6},{9,8},{10,9},{11,10},{12... | collective-permute-start | bytes 3080 | tf_op jit(solution)/shard_map/ppermute | solution.py:17
  165.1 7.2 %collective-permute-start.16 = (f32[512]{0:T(512)}, f32[512]{0:T(512)}, u32[]{:S(2)}, u32[]{:S(2)}) collective-permute-start(f32[512]{0:T(512)} %bitcast.33), channel_id=1, source_target_pairs={{8,0},{16,8},{24,16},{32,24},{40,32},{48,40},{56,48},{64,56},{72,6... | collective-permute-start | bytes 6152 | tf_op jit(solution)/shard_map/ppermute | solution.py:17
  178.4 88.2 %collective-permute-start.15 = (f32[256]{0:T(256)S(1)}, f32[256]{0:T(256)S(1)}, u32[]{:S(2)}, u32[]{:S(2)}) collective-permute-start(f32[256]{0:T(256)S(1)} %slice_reduce_fusion.8), channel_id=1, source_target_pairs={{0,1},{1,2},{2,3},{3,4},{4,5},{5,6},{6,7},{8,9},{9,10},{10,11},{11... | collective-permute-start | bytes 3080 | tf_op jit(solution)/shard_map/ppermute | solution.py:17
  184.3 82.4 %collective-permute-start.17 = (f32[512]{0:T(512)S(1)}, f32[512]{0:T(512)S(1)}, u32[]{:S(2)}, u32[]{:S(2)}) collective-permute-start(f32[512]{0:T(512)S(1)} %bitcast.187), channel_id=1, source_target_pairs={{0,8},{8,16},{16,24},{24,32},{32,40},{40,48},{48,56},{56,64},{64,7... | collective-permute-start | bytes 6152 | tf_op jit(solution)/shard_map/ppermute | solution.py:17
  376.5 12.8 %collective-permute-start.18 = (f32[512]{0:T(512)}, f32[512]{0:T(512)}, u32[]{:S(2)}, u32[]{:S(2)}) collective-permute-start(f32[512]{0:T(512)} %bitcast.45), channel_id=1, source_target_pairs={{8,0},{16,8},{24,16},{32,24},{40,32},{48,40},{56,48},{64,56},{72,6... | collective-permute-start | bytes 6152 | tf_op jit(solution)/shard_map/ppermute | solution.py:17
  397.4 8.5 %collective-permute-start.20 = (f32[256]{0:T(256)S(1)}, f32[256]{0:T(256)S(1)}, u32[]{:S(2)}, u32[]{:S(2)}) collective-permute-start(f32[256]{0:T(256)S(1)} %slice_reduce_fusion.6), channel_id=1, source_target_pairs={{0,1},{1,2},{2,3},{3,4},{4,5},{5,6},{6,7},{8,9},{9,10},{10,11},{11... | collective-permute-start | bytes 3080 | tf_op jit(solution)/shard_map/ppermute | solution.py:17
  400.4 8.3 %collective-permute-start.21 = (f32[512]{0:T(512)}, f32[512]{0:T(512)}, u32[]{:S(2)}, u32[]{:S(2)}) collective-permute-start(f32[512]{0:T(512)} %bitcast.49), channel_id=1, source_target_pairs={{0,8},{8,16},{16,24},{24,32},{32,40},{40,48},{48,56},{56,64},{64,7... | collective-permute-start | bytes 6152 | tf_op jit(solution)/shard_map/ppermute | solution.py:17
  429.5 9.9 %collective-permute-start.22 = (f32[512]{0:T(512)}, f32[512]{0:T(512)}, u32[]{:S(2)}, u32[]{:S(2)}) collective-permute-start(f32[512]{0:T(512)} %bitcast.52), channel_id=1, source_target_pairs={{8,0},{16,8},{24,16},{32,24},{40,32},{48,40},{56,48},{64,56},{72,6... | collective-permute-start | bytes 6152 | tf_op jit(solution)/shard_map/ppermute | solution.py:17
  446.5 11.9 %collective-permute-start.24 = (f32[256]{0:T(256)S(1)}, f32[256]{0:T(256)S(1)}, u32[]{:S(2)}, u32[]{:S(2)}) collective-permute-start(f32[256]{0:T(256)S(1)} %slice_reduce_fusion.4), channel_id=1, source_target_pairs={{0,1},{1,2},{2,3},{3,4},{4,5},{5,6},{6,7},{8,9},{9,10},{10,11},{11... | collective-permute-start | bytes 3080 | tf_op jit(solution)/shard_map/ppermute | solution.py:17
  451.5 8.1 %collective-permute-start.25 = (f32[512]{0:T(512)}, f32[512]{0:T(512)}, u32[]{:S(2)}, u32[]{:S(2)}) collective-permute-start(f32[512]{0:T(512)} %bitcast.56), channel_id=1, source_target_pairs={{0,8},{8,16},{16,24},{24,32},{32,40},{40,48},{48,56},{56,64},{64,7... | collective-permute-start | bytes 6152 | tf_op jit(solution)/shard_map/ppermute | solution.py:17
  480.3 9.6 %collective-permute-start.26 = (f32[512]{0:T(512)}, f32[512]{0:T(512)S(1)}, u32[]{:S(2)}, u32[]{:S(2)}) collective-permute-start(f32[512]{0:T(512)} %bitcast.59), channel_id=1, source_target_pairs={{8,0},{16,8},{24,16},{32,24},{40,32},{48,40},{56,48},{64,56},{72,6... | collective-permute-start | bytes 6152 | tf_op jit(solution)/shard_map/ppermute | solution.py:17
  497.6 10.8 %collective-permute-start.28 = (f32[256]{0:T(256)S(1)}, f32[256]{0:T(256)S(1)}, u32[]{:S(2)}, u32[]{:S(2)}) collective-permute-start(f32[256]{0:T(256)S(1)} %slice_reduce_fusion.2), channel_id=1, source_target_pairs={{0,1},{1,2},{2,3},{3,4},{4,5},{5,6},{6,7},{8,9},{9,10},{10,11},{11... | collective-permute-start | bytes 3080 | tf_op jit(solution)/shard_map/ppermute | solution.py:17
  501.5 8.2 %collective-permute-start.29 = (f32[512]{0:T(512)S(1)}, f32[512]{0:T(512)S(1)}, u32[]{:S(2)}, u32[]{:S(2)}) collective-permute-start(f32[512]{0:T(512)S(1)} %bitcast.185), channel_id=1, source_target_pairs={{0,8},{8,16},{16,24},{24,32},{32,40},{40,48},{48,56},{56,64},{64,7... | collective-permute-start | bytes 6152 | tf_op jit(solution)/shard_map/ppermute | solution.py:17
  529.1 9.4 %collective-permute-start.30 = (f32[512]{0:T(512)S(1)}, f32[512]{0:T(512)S(1)}, u32[]{:S(2)}, u32[]{:S(2)}) collective-permute-start(f32[512]{0:T(512)S(1)} %bitcast.183), channel_id=1, source_target_pairs={{8,0},{16,8},{24,16},{32,24},{40,32},{48,40},{56,48},{64,56},{72,6... | collective-permute-start | bytes 6152 | tf_op jit(solution)/shard_map/ppermute | solution.py:17
  545.2 10.6 %collective-permute-start.32 = (f32[256]{0:T(256)S(1)}, f32[256]{0:T(256)S(1)}, u32[]{:S(2)}, u32[]{:S(2)}) collective-permute-start(f32[256]{0:T(256)S(1)} %slice_reduce_fusion), channel_id=1, source_target_pairs={{0,1},{1,2},{2,3},{3,4},{4,5},{5,6},{6,7},{8,9},{9,10},{10,11},{11... | collective-permute-start | bytes 3080 | tf_op jit(solution)/shard_map/ppermute | solution.py:17
  549.0 8.1 %collective-permute-start.33 = (f32[512]{0:T(512)S(1)}, f32[512]{0:T(512)S(1)}, u32[]{:S(2)}, u32[]{:S(2)}) collective-permute-start(f32[512]{0:T(512)S(1)} %bitcast.184), channel_id=1, source_target_pairs={{0,8},{8,16},{16,24},{24,32},{32,40},{40,48},{48,56},{56,64},{64,7... | collective-permute-start | bytes 6152 | tf_op jit(solution)/shard_map/ppermute | solution.py:17
  565.9 22.3 %all-to-all-start.3 = ((f32[128,4,1]{1,2,0:T(1,128)}), f32[128,4,1]{1,2,0:T(1,128)S(1)}, u32[]{:S(2)}, u32[]{:S(2)}) async-start(f32[128,4,1]{1,2,0:T(1,128)} %bitcast.74), calls=%async_computation.3 | async-start | bytes 131072 | tf_op jit(solution)/shard_map/all_to_all | solution.py:219
  (96 other events, 986.4 us)
where the time goes:
time: 601 us; the launch traced here: 592 us
  local copies, waits for them, and re-layouts  181 us (30%)
  other arithmetic  153 us (25%)
  starting transfers between devices  140 us (23%)
  blocking collectives  71.3 us (12%)
  waiting for transfers between devices  43.3 us (7%)
    ppermute x34, starting transfers between devices, shifted(): return lax.ppermute(shard, axis, pairs)  108 us
    gather x4, local copies, waits for them, and re-layouts, body(): gathered.append(surface[safe_row, safe_col] * owned_weight)  92.9 us
    psum x1, blocking collectives, body(): lax.psum(local_read, ('gx', 'gy'))  71.3 us
    unnamed x7, other arithmetic  62.3 us
    div x5, other arithmetic, face_flux(): return wet_here * wet_there * pushed / drag_factor  20.3 us
    add_any x4, other arithmetic, face_flux(): depth_here + here + depth_there + there  19.4 us
    unnamed x185, local copies, waits for them, and re-layouts  14.6 us
    all_to_all x1, starting transfers between devices, body(): lax.all_to_all(per_slot, ('gx', 'gy'), split_axis=0, concat_axis=0, tiled...  12.4 us
  transfers between devices with their start and end apart: 38, of which 12 were waited for; matrix products, arithmetic and copies ran while one was open for 26% of the time, Pallas kernels for 0%

commit v1 on v0

v1 whole, which is shorter than its diff:
```python
import math

import jax
import jax.numpy as jnp
from jax import lax
from jax.experimental import pallas as pl
from jax.experimental.pallas import tpu as pltpu
from jax.sharding import PartitionSpec as P

wave_gain = 0.2
mass_gain = 0.2
min_depth = 0.25
speed_floor = 0.01

HALO = 8
CHUNK = 33
SLOTS = 4
LN2 = math.log(2.0)
F32 = jnp.float32
I32 = jnp.int32


def vmem():
    return pl.BlockSpec(memory_space=pltpu.VMEM)


def smem():
    return pl.BlockSpec(memory_space=pltpu.SMEM)


def hbm():
    return pl.BlockSpec(memory_space=pl.ANY)


def shifted(shard, axis, by):
    devices = lax.axis_size(axis)
    pairs = [(i, i + by) for i in range(devices) if 0 <= i + by < devices]
    return lax.ppermute(shard, axis, pairs)


def pack_kernel(row_ref, slip_ref, pattern_ref, meta_ref, out_ref):
    rows = out_ref.shape[0]
    entries = pattern_ref.shape[0]
    per_fault = entries // slip_ref.shape[0]
    zero = jnp.zeros((8, 128), F32)

    def clear(i, c):
        out_ref[pl.ds(pl.multiple_of(i * 8, 8), 8), :] = zero
        return c

    lax.fori_loop(0, rows // 8, clear, 0, unroll=16)
    for t in range(rows // CHUNK):
        out_ref[pl.ds(t * CHUNK + 32, 1), :] = meta_ref[pl.ds(t, 1), :]

    def place(s, c):
        slip = slip_ref[s]
        for j in range(per_fault):
            i = s * per_fault + j
            out_ref[pl.ds(row_ref[i], 8), :] = pattern_ref[i] * slip
        return c

    lax.fori_loop(0, slip_ref.shape[0], place, 0)


def edges_of(first, last):
    lane = lax.broadcasted_iota(I32, first.shape, 1)
    both = jnp.where(lane < 64, first, last).T
    return both[0:8], both[120:128]


def side_block(east, west):
    rows = east.shape[1]
    gap = jnp.zeros((128 - 16, rows), F32)
    return jnp.concatenate([east, gap, west], axis=0).T


def scatter_kernel(block_ref, recv_ref, wet_ref, eta_ref, west_ref, east_ref, *acc):
    tiles = recv_ref.shape[0] // CHUNK
    rows, cols = eta_ref.shape
    across = cols // 128
    zero = jnp.zeros((8, 128), F32)

    def clear(i, c):
        for a in acc:
            a[i] = zero
        return c

    lax.fori_loop(0, acc[0].shape[0], clear, 0, unroll=8)

    def add(t, c):
        for j in range(SLOTS):
            b = block_ref[t * SLOTS + j]
            acc[j][b] = acc[j][b] + recv_ref[pl.ds(t * CHUNK + 8 * j, 8), :]
        return c

    lax.fori_loop(0, tiles, add, 0, unroll=4)

    def merge(i, c):
        r = pl.multiple_of(i * 8, 8)
        for q in range(across):
            b = i * across + q
            total = (acc[0][b] + acc[1][b]) + (acc[2][b] + acc[3][b])
            wet = wet_ref[pl.ds(r, 8), q * 128 : q * 128 + 128].astype(F32)
            eta_ref[pl.ds(r, 8), q * 128 : q * 128 + 128] = total * wet
        return c

    lax.fori_loop(0, rows // 8, merge, 0, unroll=2)
    west, east = edges_of(eta_ref[:, 0:128], eta_ref[:, cols - 128 : cols])
    west_ref[...] = west
    east_ref[...] = east


def static_edge_kernel(depth_ref, wet_ref, fric_ref, west_ref, east_ref):
    cols = depth_ref.shape[1]
    for n, ref in enumerate((depth_ref, wet_ref, fric_ref)):
        west, east = edges_of(ref[:, 0:128].astype(F32), ref[:, cols - 128 : cols].astype(F32))
        west_ref[8 * n : 8 * n + 8] = west
        east_ref[8 * n : 8 * n + 8] = east


def rim_kernel(*refs):
    fields = refs[:-4]
    east_ref, west_ref, top_ref, bottom_ref = refs[-4:]
    rows, cols = fields[0].shape
    for n, ref in enumerate(fields):
        block = side_block(east_ref[8 * n : 8 * n + 8], west_ref[8 * n : 8 * n + 8])
        top_ref[8 * n : 8 * n + 8, 0:cols] = ref[0:8, :].astype(F32)
        top_ref[8 * n : 8 * n + 8, cols:] = block[0:8]
        bottom_ref[8 * n : 8 * n + 8, 0:cols] = ref[rows - 8 : rows, :].astype(F32)
        bottom_ref[8 * n : 8 * n + 8, cols:] = block[rows - 8 : rows]


def assemble(out, n, ref, east_ref, west_ref, north_ref, south_ref):
    rows, cols = ref.shape
    out[0:8, :] = north_ref[8 * n : 8 * n + 8]
    out[8 : 8 + rows, 0:cols] = ref[...].astype(F32)
    out[8 : 8 + rows, cols:] = side_block(
        east_ref[8 * n : 8 * n + 8], west_ref[8 * n : 8 * n + 8]
    )
    out[8 + rows : 16 + rows, :] = south_ref[8 * n : 8 * n + 8]


def row_iota(shape):
    return lax.broadcasted_iota(I32, shape, 0)


def face_static_kernel(
    depth_ref, wet_ref, fric_ref, east_ref, west_ref, north_ref, south_ref,
    wet_out, dde, dds, rre, rrs, wwe, wws, depth_x, fric_x,
):
    halos = (east_ref, west_ref, north_ref, south_ref)
    assemble(depth_x, 0, depth_ref, *halos)
    assemble(wet_out, 1, wet_ref, *halos)
    assemble(fric_x, 2, fric_ref, *halos)
    rows, cols = depth_x.shape
    last = row_iota((8, cols)) == 7

    def step(i, c):
        r = pl.multiple_of(i * 8, 8)
        n = pl.multiple_of(jnp.minimum(r + 8, rows - 8), 8)
        for src, e_out, s_out, half in (
            (depth_x, dde, dds, True),
            (fric_x, rre, rrs, True),
            (wet_out, wwe, wws, False),
        ):
            here = src[pl.ds(r, 8), :]
            nxt = src[pl.ds(n, 8), :]
            east = pltpu.roll(here, cols - 1, 1)
            south = jnp.where(last, pltpu.roll(nxt, 7, 0), pltpu.roll(here, 7, 0))
            if half:
                e_out[pl.ds(r, 8), :] = 0.5 * (here + east)
                s_out[pl.ds(r, 8), :] = 0.5 * (here + south)
            else:
                e_out[pl.ds(r, 8), :] = here * east
                s_out[pl.ds(r, 8), :] = here * south
        return c

    lax.fori_loop(0, rows // 8, step, 0)


def gauge_kernel(place_ref, row_ref, col_ref, obs_ref, count_out, obs_out):
    steps, rows, cols = obs_out.shape
    own_rows = rows - 2 * HALO
    own_cols = cols - 128
    gx, gy, wx, wy = place_ref[0], place_ref[1], place_ref[2], place_ref[3]
    per = row_ref.shape[0] // (wx * wy)
    zero = jnp.zeros((8, cols), F32)

    def clear(i, c):
        r = pl.multiple_of(i * 8, 8)
        count_out[pl.ds(r, 8), :] = zero
        for k in range(steps):
            obs_out[k, pl.ds(r, 8), :] = zero
        return c

    lax.fori_loop(0, rows // 8, clear, 0)
    sub = row_iota((8, 128))
    lane = lax.broadcasted_iota(I32, (8, 128), 1)

    for dx in (-1, 0, 1):
        for dy in (-1, 0, 1):
            tx = gx + dx
            ty = gy + dy
            inside = (tx >= 0) & (tx < wx) & (ty >= 0) & (ty < wy)
            first = jnp.where(inside, (tx * wy + ty) * per, 0)

            def one(g, c, first=first, inside=inside):
                r = row_ref[first + g] - gx * own_rows + HALO
                q = col_ref[first + g] - gy * own_cols
                ok = inside & (r >= 0) & (r < rows) & (q >= -HALO) & (q < own_cols + HALO)
                q = jnp.where(q < 0, q + cols, q)

                @pl.when(ok)
                def _():
                    rb = pl.multiple_of(r // 8 * 8, 8)
                    cb = pl.multiple_of(q // 128 * 128, 128)
                    hit = (sub == r % 8) & (lane == q % 128)
                    at = (pl.ds(rb, 8), pl.ds(cb, 128))
                    count_out[at] = count_out[at] + jnp.where(hit, 1.0, 0.0)
                    for k in range(steps):
                        at_k = (k,) + at
                        obs_out[at_k] = obs_out[at_k] + jnp.where(hit, obs_ref[k, first + g], 0.0)

                return c

            lax.fori_loop(0, per, one, 0)


def face(f, s, sn, dd, rr, ww):
    x = dd + 0.5 * (s + sn)
    total = jnp.maximum(x, min_depth)
    diff = sn - s
    push = (-wave_gain) * (total * diff)
    if f is not None:
        push = push + f
    t = push * push + speed_floor
    rs = lax.rsqrt(t)
    log = jnp.log(total)
    rw = rr * jnp.exp2(log * (-7.0 / 3.0 / LN2))
    z = rw * (t * rs)
    inv = 1.0 / (1.0 + z)
    wi = ww * inv
    flux = wi * push
    a = wi * inv * (1.0 + speed_floor * (rw * rs))
    depth_part = (flux * inv) * (z * jnp.exp2(log * (-1.0 / LN2))) * (7.0 / 3.0)
    ga = wave_gain * a
    half = jnp.where(x > min_depth, 0.5, jnp.where(x == min_depth, 0.25, 0.0))
    u = half * (depth_part - ga * diff)
    v = ga * total
    return flux, a, u + v, u - v


def merge_rows(tiles):
    sub = row_iota((8, 128))
    for width in (1, 2, 4):
        low = (sub & width) == 0
        tiles = [
            jnp.where(low, p, q) + pltpu.roll(jnp.where(low, q, p), width, 0)
            for p, q in zip(tiles[0::2], tiles[1::2])
        ]
    return tiles[0]


def solve_kernel(
    place_ref, grow_ref, gcol_ref, block_ref,
    eta_ref, east_ref, west_ref, north_ref, south_ref,
    wet, dde, dds, rre, rrs, wwe, wws,
    count_hbm, obs_hbm, recv_hbm,
    final_ref, adj_ref, back_ref,
    surf, fe, fs, ae, pe, qe, as_, ps, qs, adj, ce, cs,
    count, obs, recv, parts, reads, sems,
):
    steps, rows, cols = obs.shape
    own_rows, own_cols = eta_ref.shape
    copies = [
        pltpu.make_async_copy(count_hbm, count, sems.at[0]),
        pltpu.make_async_copy(obs_hbm, obs, sems.at[1]),
        pltpu.make_async_copy(recv_hbm, recv, sems.at[2]),
    ]
    for c in copies:
        c.start()
    start = surf.at[0]
    assemble(start, 0, eta_ref, east_ref, west_ref, north_ref, south_ref)
    sub = row_iota((8, cols))
    last = sub == 7
    firstrow = sub == 0
    blocks = rows // 8

    def nxt(i):
        return pl.multiple_of(jnp.minimum(i * 8 + 8, rows - 8), 8)

    for k in range(steps):

        def forward(i, carry, k=k):
            s, s_up, f_down = carry
            r = pl.multiple_of(i * 8, 8)
            here = pl.ds(r, 8)
            sn = surf[k, pl.ds(nxt(i), 8), :]
            sn_up = pltpu.roll(sn, 7, 0)
            s_south = jnp.where(last, sn_up, s_up)
            s_east = pltpu.roll(s, cols - 1, 1)
            old_e = None if k == 0 else fe[here, :]
            old_s = None if k == 0 else fs[here, :]
            flux, a, p, q = face(old_e, s, s_east, dde[here, :], rre[here, :], wwe[here, :])
            fe[here, :] = flux
            if k > 0:
                ae[k - 1, here, :] = a
            pe[k, here, :] = p
            qe[k, here, :] = q
            div = flux - pltpu.roll(flux, 1, 1)
            flux, a, p, q = face(old_s, s, s_south, dds[here, :], rrs[here, :], wws[here, :])
            fs[here, :] = flux
            if k > 0:
                as_[k - 1, here, :] = a
            ps[k, here, :] = p
            qs[k, here, :] = q
            down = pltpu.roll(flux, 1, 0)
            div = div + (flux - jnp.where(firstrow, f_down, down))
            surf[k + 1, here, :] = wet[here, :] * (s - mass_gain * div)
            return sn, sn_up, down

        s0 = surf[k, 0:8, :]
        lax.fori_loop(
            0, blocks, forward, (s0, pltpu.roll(s0, 7, 0), jnp.zeros((8, cols), F32))
        )

    final_ref[...] = surf[steps, HALO : HALO + own_rows, 0:own_cols]

    gx, gy = place_ref[0], place_ref[1]
    lane8 = lax.broadcasted_iota(I32, (8, 128), 1)
    sub8 = row_iota((8, 128))
    per = grow_ref.shape[0] // (place_ref[2] * place_ref[3])
    per_tile = reads.shape[0] // steps
    first = (gx * place_ref[3] + gy) * per
    for g0 in range(0, per_tile, 8):
        spots = []
        for g in range(g0, g0 + 8):
            r = jnp.clip(grow_ref[first + g] - gx * own_rows, 0, own_rows - 1) + HALO
            q = jnp.clip(gcol_ref[first + g] - gy * own_cols, 0, own_cols - 1)
            at = (
                pl.ds(pl.multiple_of(r // 8 * 8, 8), 8),
                pl.ds(pl.multiple_of(q // 128 * 128, 128), 128),
            )
            spots.append((at, (sub8 == r % 8) & (lane8 == q % 128)))
        for k in range(steps):
            picked = [jnp.where(hit, surf[(k + 1,) + at], 0.0) for at, hit in spots]
            reads[k * per_tile + g0 : k * per_tile + g0 + 8, :] = merge_rows(picked)
    values = jnp.sum(reads[...], axis=1, keepdims=True)
    spots = row_iota(reads.shape) + SLOTS == lax.broadcasted_iota(I32, reads.shape, 1)
    reading_row = jnp.sum(jnp.where(spots, values, 0.0), axis=0, keepdims=True)

    for c in copies:
        c.wait()

    for k in reversed(range(steps)):

        def seeded(value, at, k):
            seed = count[at, :] * surf[k + 1, at, :] - obs[k, at, :]
            return seed if value is None else value + seed

        def b_of(r, k=k):
            at = pl.ds(r, 8)
            a = seeded(None, at, k) if k == steps - 1 else adj[at, :]
            return wet[at, :] * a

        def backward(i, carry, k=k):
            b, b_up, x_down = carry
            r = pl.multiple_of(i * 8, 8)
            here = pl.ds(r, 8)
            bn = b_of(nxt(i))
            bn_up = pltpu.roll(bn, 7, 0)
            b_south = jnp.where(last, bn_up, b_up)
            b_east = pltpu.roll(b, cols - 1, 1)
            ge = mass_gain * (b_east - b)
            gs = mass_gain * (b_south - b)
            if k < steps - 1:
                ge = ge + ce[here, :]
                gs = gs + cs[here, :]
            if k > 0:
                ce[here, :] = ge * ae[k - 1, here, :]
                cs[here, :] = gs * as_[k - 1, here, :]
            xe = ge * qe[k, here, :]
            xs = gs * qs[k, here, :]
            down = pltpu.roll(xs, 1, 0)
            out = b + ge * pe[k, here, :] + pltpu.roll(xe, 1, 1)
            out = out + gs * ps[k, here, :] + jnp.where(firstrow, x_down, down)
            if k > 0:
                out = seeded(out, here, k - 1)
            adj[here, :] = out
            return bn, bn_up, down

        b0 = b_of(0)
        lax.fori_loop(
            0, blocks, backward, (b0, pltpu.roll(b0, 7, 0), jnp.zeros((8, cols), F32))
        )

    adj_ref[...] = adj[HALO : HALO + own_rows, 0:own_cols]

    across = own_cols // 128
    tiles = recv.shape[0] // CHUNK

    def sens(i, c):
        for j in range(SLOTS):
            products = []
            for u in range(8):
                t = i * 8 + u
                b = block_ref[t * SLOTS + j]
                rb = pl.multiple_of(b // across * 8 + HALO, 8)
                cb = pl.multiple_of(b % across * 128, 128)
                at = (pl.ds(rb, 8), pl.ds(cb, 128))
                products.append(
                    (adj[at] * wet[at]) * recv[pl.ds(t * CHUNK + 8 * j, 8), :]
                )
            parts[j, pl.ds(pl.multiple_of(i * 8, 8), 8), :] = merge_rows(products)
        return c

    lax.fori_loop(0, tiles // 8, sens, 0)
    lanes = lax.broadcasted_iota(I32, (tiles, 128), 1)
    out = jnp.broadcast_to(reading_row, (tiles, 128))
    for j in range(SLOTS):
        out = jnp.where(lanes == j, jnp.sum(parts[j], axis=1, keepdims=True), out)
    back_ref[...] = out


def body(
    ocean_depth,
    wet_mask,
    manning,
    fault_slip,
    pattern,
    foot_tile,
    foot_block,
    gauge_row,
    gauge_col,
    observed,
):
    rows_here, cols_here = ocean_depth.shape
    steps, gauges = observed.shape
    width_x = lax.axis_size("gx")
    width_y = lax.axis_size("gy")
    devices = width_x * width_y
    entries = pattern.shape[0]
    faults = fault_slip.shape[0]
    per_fault = entries // faults
    per_tile = gauges // devices
    both = ("gx", "gy")
    rows, cols = rows_here + 2 * HALO, cols_here + 128
    f = jax.ShapeDtypeStruct

    target = foot_tile[:, 0]
    order = jnp.arange(entries, dtype=I32)
    earlier = (target[:, None] == target[None, :]) & (order[:, None] > order[None, :])
    rank = jnp.sum(earlier.astype(I32), axis=1)
    hot_tile = (jnp.arange(devices, dtype=I32)[:, None] == target[None, :]).astype(jnp.bfloat16)
    lane = jnp.arange(128, dtype=I32)[None, :]
    hot_slot = jnp.where(lane == rank[:, None], foot_block[:, None] + 1, 0)
    hot_fault = jnp.where(lane == rank[:, None] + 8, order[:, None] // per_fault + 1, 0)
    table = jnp.dot(
        hot_tile, (hot_slot + hot_fault).astype(jnp.bfloat16), preferred_element_type=F32
    )
    packed = pl.pallas_call(
        pack_kernel,
        out_shape=f((devices * CHUNK, 128), F32),
        in_specs=[smem(), smem(), vmem(), vmem()],
        out_specs=vmem(),
        name="pack",
    )(target * CHUNK + 8 * rank, fault_slip, pattern, table)
    recv = lax.all_to_all(packed.reshape(-1), both, split_axis=0, concat_axis=0, tiled=True)
    block_index = jnp.maximum(
        recv.reshape(devices, CHUNK * 128)[:, 4096 : 4096 + SLOTS].astype(I32) - 1, 0
    ).reshape(-1)
    recv = recv.reshape(devices * CHUNK, 128)

    west, east = pl.pallas_call(
        static_edge_kernel,
        out_shape=[f((24, rows_here), F32)] * 2,
        in_specs=[vmem()] * 3,
        out_specs=[vmem()] * 2,
        name="static_edges",
    )(ocean_depth, wet_mask, manning)
    from_east = shifted(west, "gy", -1)
    from_west = shifted(east, "gy", 1)
    top, bottom = pl.pallas_call(
        rim_kernel,
        out_shape=[f((24, cols), F32)] * 2,
        in_specs=[vmem()] * 5,
        out_specs=[vmem()] * 2,
        name="static_rims",
    )(ocean_depth, wet_mask, manning, from_east, from_west)
    from_south = shifted(top, "gx", -1)
    from_north = shifted(bottom, "gx", 1)
    grid = f((rows, cols), F32)
    faces = pl.pallas_call(
        face_static_kernel,
        out_shape=[grid] * 7,
        in_specs=[vmem()] * 7,
        out_specs=[vmem()] * 7,
        scratch_shapes=[pltpu.VMEM((rows, cols), F32)] * 2,
        name="faces",
    )(ocean_depth, wet_mask, manning, from_east, from_west, from_north, from_south)
    place = jnp.stack(
        [lax.axis_index("gx"), lax.axis_index("gy"), jnp.int32(width_x), jnp.int32(width_y)]
    ).astype(I32)
    count, obs = pl.pallas_call(
        gauge_kernel,
        out_shape=[grid, f((steps, rows, cols), F32)],
        in_specs=[smem()] * 4,
        out_specs=[vmem()] * 2,
        name="gauges",
    )(place, gauge_row, gauge_col, observed)

    eta, west, east = pl.pallas_call(
        scatter_kernel,
        out_shape=[f((rows_here, cols_here), F32)] + [f((8, rows_here), F32)] * 2,
        in_specs=[smem(), vmem(), vmem()],
        out_specs=[vmem()] * 3,
        scratch_shapes=[pltpu.VMEM((rows_here * cols_here // 1024, 8, 128), F32)] * SLOTS,
        name="scatter",
    )(block_index, recv, wet_mask)
    from_east = shifted(west, "gy", -1)
    from_west = shifted(east, "gy", 1)
    top, bottom = pl.pallas_call(
        rim_kernel,
        out_shape=[f((8, cols), F32)] * 2,
        in_specs=[vmem()] * 3,
        out_specs=[vmem()] * 2,
        name="eta_rims",
    )(eta, from_east, from_west)
    from_south = shifted(top, "gx", -1)
    from_north = shifted(bottom, "gx", 1)

    tile = f((rows_here, cols_here), F32)
    scratch = pltpu.VMEM((rows, cols), F32)
    final, adjoint, back = pl.pallas_call(
        solve_kernel,
        out_shape=[tile, tile, f((devices, 128), F32)],
        in_specs=[smem()] * 4 + [vmem()] * 12 + [hbm()] * 3,
        out_specs=[vmem()] * 3,
        scratch_shapes=[
            pltpu.VMEM((steps + 1, rows, cols), F32),
            scratch,
            scratch,
            pltpu.VMEM((steps - 1, rows, cols), F32),
            pltpu.VMEM((steps, rows, cols), F32),
            pltpu.VMEM((steps, rows, cols), F32),
            pltpu.VMEM((steps - 1, rows, cols), F32),
            pltpu.VMEM((steps, rows, cols), F32),
            pltpu.VMEM((steps, rows, cols), F32),
            scratch,
            scratch,
            scratch,
            scratch,
            pltpu.VMEM((steps, rows, cols), F32),
            pltpu.VMEM((devices * CHUNK, 128), F32),
            pltpu.VMEM((SLOTS, devices, 128), F32),
            pltpu.VMEM((steps * per_tile, 128), F32),
            pltpu.SemaphoreType.DMA((3,)),
        ],
        name="solve",
    )(
        place, gauge_row, gauge_col, block_index,
        eta, from_east, from_west, from_north, from_south,
        *faces, count, obs, recv,
    )
    returned = lax.all_to_all(back, both, split_axis=0, concat_axis=0, tiled=True)
    readings = (
        returned[:, SLOTS : SLOTS + steps * per_tile]
        .reshape(devices, steps, per_tile)
        .transpose(1, 0, 2)
        .reshape(steps, gauges)
    )
    fault_of = table[:, 8 : 8 + SLOTS].astype(I32) - 1
    mine = fault_of[:, :, None] == jnp.arange(faults, dtype=I32)[None, None, :]
    grad_slip = (
        jnp.sum(jnp.where(mine, returned[:, :SLOTS, None], 0.0), axis=(0, 1)) / fault_slip
    )
    return (final, readings, adjoint, grad_slip)


def solution(mesh):
    placed = (
        P("gx", "gy"),
        P("gx", "gy"),
        P("gx", "gy"),
        P(("gx", "gy")),
        P(("gx", "gy"), None, None),
        P(("gx", "gy"), None),
        P(("gx", "gy")),
        P(),
        P(),
        P(),
    )
    return jax.shard_map(
        body,
        mesh=mesh,
        in_specs=placed,
        out_specs=(P("gx", "gy"), P(), P("gx", "gy"), P(("gx", "gy"))),
        check_vma=False,
    )
```

time: 601 us -> 176 us (0.29); the launches traced: 592 us -> 175 us
  local copies, waits for them, and re-layouts: 181 us -> 10.2 us
  other arithmetic: 153 us -> 4.86 us
  starting transfers between devices: 140 us -> 44.9 us
  Pallas kernels: 0 us -> 80.5 us
  blocking collectives: 71.3 us -> 0 us
  waiting for transfers between devices: 43.3 us -> 32.5 us
    gather x7 -> x0, local copies, waits for them, and re-layouts: 101 us -> none  [the longest x4 92.9 us: body(): gathered.append(surface[safe_row, safe_col] * owned_weight)]
    ppermute x34 -> x8, starting transfers between devices: 108 us -> 24.4 us  [shifted(): return lax.ppermute(shard, axis, pairs)]
    pallas_call x0 -> x8, Pallas kernels: none -> 80.5 us  [the longest x1 53.8 us: body(): pl.pallas_call(solve_kernel, out_shape=[tile, tile, f((devices, 128), F32...]
    psum x1 -> x0, blocking collectives: 71.3 us -> none  [body(): lax.psum(local_read, ('gx', 'gy'))]
    unnamed x7 -> x0, other arithmetic: 62.3 us -> none
    add_any x5 -> x0, other arithmetic: 20.5 us -> none  [the longest x4 19.4 us: face_flux(): depth_here + here + depth_there + there]
    div x5 -> x1, other arithmetic: 20.3 us -> 0.52 us  [body(): jnp.sum(jnp.where(mine, returned[:, :SLOTS, None], 0.0), axis=(0, 1))]
    slice x33 -> x2, local copies, waits for them, and re-layouts: 19 us -> 0.01 us  [the longest x1 0.01 us: body(): returned[:, SLOTS:SLOTS + steps * per_tile]]
  transfers between devices with their start and end apart: 38 -> 10, of which waited for: 12 -> 2; matrix products, arithmetic and copies ran while one was open for 26% -> 4% of each run, Pallas kernels for 0% -> 13%
where the time goes in v1:
time: 176 us; the launch traced here: 175 us
  Pallas kernels  80.5 us (46%)
  starting transfers between devices  44.9 us (26%)
  waiting for transfers between devices  32.5 us (18%)
  local copies, waits for them, and re-layouts  10.2 us (6%)
  other arithmetic  4.86 us (3%)
    pallas_call x1, Pallas kernels, body(): pl.pallas_call(solve_kernel, out_shape=[tile, tile, f((devices, 128), F32...  53.8 us
    ppermute x8, starting transfers between devices, shifted(): return lax.ppermute(shard, axis, pairs)  24.4 us
    all_to_all x1, waiting for transfers between devices, body(): lax.all_to_all(packed.reshape(-1), both, split_axis=0, concat_axis=0, til...  22.8 us
    all_to_all x1, starting transfers between devices, body(): lax.all_to_all(packed.reshape(-1), both, split_axis=0, concat_axis=0, til...  11.5 us
    all_to_all x1, waiting for transfers between devices, body(): lax.all_to_all(back, both, split_axis=0, concat_axis=0, tiled=True)  9.72 us
    all_to_all x1, starting transfers between devices, body(): lax.all_to_all(back, both, split_axis=0, concat_axis=0, tiled=True)  9.03 us
    pallas_call x1, Pallas kernels, body(): pl.pallas_call(gauge_kernel, out_shape=[grid, f((steps, rows, cols), F32)...  7.01 us
    pallas_call x1, Pallas kernels, body(): pl.pallas_call(face_static_kernel, out_shape=[grid] * 7, in_specs=[vmem()...  6.77 us
  transfers between devices with their start and end apart: 10, of which 2 were waited for; matrix products, arithmetic and copies ran while one was open for 4% of the time, Pallas kernels for 13%

profile of v1, /device:TPU:1, one launch (start us, length us, event | category | flops | bytes accessed | tf_op | source)
XLA Modules:
  0.0 174.8 jit_solution(12225433178311395218)
XLA Ops:
  0.6 0.9 convert_reduce_fusion
  1.6 1.3 broadcast_add_fusion.1
  2.8 0.7 fusion.11
  3.5 1.1 fusion.1
  4.6 0.7 copy.35.meta_ref
  5.3 3.1 %pack.1 = f32[4224,128]{1,0:T(8,128)} custom-call(s32[256]{0:T(256)} %get-tuple-element.47.row_ref, f32[16]{0:T(128)} %slip_ref.1, f32[256,8,128]{2,1,0:T(8,128)} %pattern_ref.1, f32[128,128]{1,0:T(8,128)} %copy.35.meta_ref), custom_call_target="tpu_custom_call" | custom-call | tf_op jit(solution)/shard_map/pack/pallas_call | solution.py:461
  8.4 11.5 %all-to-all-start = ((f32[128,4224,1]{1,2,0:T(1,128)}), f32[128,4224,1]{1,2,0:T(1,128)S(1)}, u32[]{:S(2)}, u32[]{:S(2)}) async-start(f32[128,4224,1]{1,2,0:T(1,128)} %bitcast.15), calls=%async_computation | async-start | bytes 4325376 | tf_op jit(solution)/shard_map/all_to_all | solution.py:468
  19.9 2.1 %static_edges.1 = (f32[24,256]{1,0:T(8,128)}, f32[24,256]{1,0:T(8,128)}) custom-call(f32[256,512]{1,0:T(8,128)} %depth_ref.3, s32[256,512]{1,0:T(8,128)} %wet_ref.5, f32[256,512]{1,0:T(8,128)} %fric_ref.3), custom_call_target="tpu_custom_call" | custom-call | tf_op jit(solution)/shard_map/static_edges/pallas_call | solution.py:474
  22.0 1.3 collective-permute-start.4
  23.3 4.0 %collective-permute-start.5 = (f32[24,256]{1,0:T(8,128)}, f32[24,256]{1,0:T(8,128)S(1)}, u32[]{:S(2)}, u32[]{:S(2)}) collective-permute-start(f32[24,256]{1,0:T(8,128)} %get-tuple-element.31), channel_id=1, source_target_pairs={{0,1},{1,2},{2,3},{3,4},{4,5},{5,6},{6,7},{8,9},{9,10},{10,11},{11... | collective-permute-start | bytes 73736 | tf_op jit(solution)/shard_map/ppermute | solution.py:38
  27.3 22.8 %all-to-all-done = f32[128,4224,1]{1,2,0:T(1,128)S(1)} async-done(((f32[128,4224,1]{1,2,0:T(1,128)}), f32[128,4224,1]{1,2,0:T(1,128)S(1)}, u32[]{:S(2)}, u32[]{:S(2)}) %all-to-all-start) | async-done | bytes 2162720 | tf_op jit(solution)/shard_map/all_to_all | solution.py:468
  50.1 4.0 %copy.37 = f32[128,4224,1]{0,1,2:T(8,128)} copy(f32[128,4224,1]{1,2,0:T(1,128)S(1)} %all-to-all-done) | data formatting | bytes 4325376 | tf_op jit(solution)/shard_map/all_to_all | solution.py:468
  54.2 0.7 fusion.10
  55.0 0.7 reshape.81.block_ref
  55.7 3.7 %scatter.1 = (f32[256,512]{1,0:T(8,128)}, f32[8,256]{1,0:T(8,128)}, f32[8,256]{1,0:T(8,128)}) custom-call(s32[512]{0:T(512)} %reshape.81.block_ref, f32[4224,128]{1,0:T(8,128)} %bitcast.13, s32[256,512]{1,0:T(8,128)} %wet_ref.5), custom_call_target="tpu_custom_call" | custom-call | tf_op jit(solution)/shard_map/scatter/pallas_call | solution.py:512
  59.3 1.3 collective-permute-start
  60.6 4.0 %collective-permute-start.1 = (f32[8,256]{1,0:T(8,128)}, f32[8,256]{1,0:T(8,128)S(1)}, u32[]{:S(2)}, u32[]{:S(2)}) collective-permute-start(f32[8,256]{1,0:T(8,128)} %get-tuple-element.27), channel_id=1, source_target_pairs={{0,1},{1,2},{2,3},{3,4},{4,5},{5,6},{6,7},{8,9},{9,10},{10,11},{11... | collective-permute-start | bytes 24584 | tf_op jit(solution)/shard_map/ppermute | solution.py:38
  65.9 2.2 %static_rims.1 = (f32[24,640]{1,0:T(8,128)}, f32[24,640]{1,0:T(8,128)}) custom-call(f32[256,512]{1,0:T(8,128)} %depth_ref.3, s32[256,512]{1,0:T(8,128)} %wet_ref.5, f32[256,512]{1,0:T(8,128)} %fric_ref.3, f32[24,256]{1,0:T(8,128)} %copy-done.1, f32[24,256]{1,0:T(8,128)} %copy-done.2), custom_call_target="tpu_custom_call" | custom-call | tf_op jit(solution)/shard_map/static_rims/pallas_call | solution.py:483
  68.0 4.8 %collective-permute-start.6 = (f32[24,640]{1,0:T(8,128)}, f32[24,640]{1,0:T(8,128)S(1)}, u32[]{:S(2)}, u32[]{:S(2)}) collective-permute-start(f32[24,640]{1,0:T(8,128)} %get-tuple-element.32), channel_id=1, source_target_pairs={{0,8},{8,16},{16,24},{24,32},{32,40},{40,48},{48,56},{56,64},{64,7... | collective-permute-start | bytes 184328 | tf_op jit(solution)/shard_map/ppermute | solution.py:38
  72.9 1.9 %collective-permute-start.7 = (f32[24,640]{1,0:T(8,128)}, f32[24,640]{1,0:T(8,128)S(1)}, u32[]{:S(2)}, u32[]{:S(2)}) collective-permute-start(f32[24,640]{1,0:T(8,128)} %get-tuple-element.33), channel_id=1, source_target_pairs={{8,0},{16,8},{24,16},{32,24},{40,32},{48,40},{56,48},{64,56},{72,6... | collective-permute-start | bytes 184328 | tf_op jit(solution)/shard_map/ppermute | solution.py:38
  75.4 1.8 %eta_rims.1 = (f32[8,640]{1,0:T(8,128)}, f32[8,640]{1,0:T(8,128)}) custom-call(f32[256,512]{1,0:T(8,128)} %get-tuple-element.25.refs_0_.eta_ref, f32[8,256]{1,0:T(8,128)} %copy-done.5, f32[8,256]{1,0:T(8,128)} %copy-done.6), custom_call_target="tpu_custom_call" | custom-call | tf_op jit(solution)/shard_map/eta_rims/pallas_call | solution.py:522
  77.2 5.1 %collective-permute-start.2 = (f32[8,640]{1,0:T(8,128)}, f32[8,640]{1,0:T(8,128)S(1)}, u32[]{:S(2)}, u32[]{:S(2)}) collective-permute-start(f32[8,640]{1,0:T(8,128)} %get-tuple-element.28), channel_id=1, source_target_pairs={{0,8},{8,16},{16,24},{24,32},{32,40},{40,48},{48,56},{56,64},{64,7... | collective-permute-start | bytes 61448 | tf_op jit(solution)/shard_map/ppermute | solution.py:38
  82.3 1.9 %collective-permute-start.3 = (f32[8,640]{1,0:T(8,128)}, f32[8,640]{1,0:T(8,128)S(1)}, u32[]{:S(2)}, u32[]{:S(2)}) collective-permute-start(f32[8,640]{1,0:T(8,128)} %get-tuple-element.29), channel_id=1, source_target_pairs={{8,0},{16,8},{24,16},{32,24},{40,32},{48,40},{56,48},{64,56},{72,6... | collective-permute-start | bytes 61448 | tf_op jit(solution)/shard_map/ppermute | solution.py:38
  84.2 0.7 pad_add_fusion.place_ref
  84.9 7.0 %gauges.1 = (f32[272,640]{1,0:T(8,128)}, f32[4,272,640]{2,1,0:T(8,128)}) custom-call(s32[4]{0:T(128)} %pad_add_fusion.place_ref, s32[2048]{0:T(1024)} %grow_ref.1, s32[2048]{0:T(1024)} %gcol_ref.1, f32[4,2048]{1,0:T(4,128)} %obs_ref.1), custom_call_target="tpu_custom_call" | custom-call | tf_op jit(solution)/shard_map/gauges/pallas_call | solution.py:504
  91.9 0.6 copy-done.3
  92.6 0.6 copy-done.4
  93.2 6.8 %faces.1 = (f32[272,640]{1,0:T(8,128)}, f32[272,640]{1,0:T(8,128)}, f32[272,640]{1,0:T(8,128)}, f32[272,640]{1,0:T(8,128)}, f32[272,640]{1,0:T(8,128)}, /*index=5*/f32[272,640]{1,0:T(8,128)}, f32[272,640]{1,0:T(8,128)}) custom-call(f32[256,512]{1,0:T(8,128)} %depth_ref.3, s32[256,512]{1,0:T(8,128)} %wet_ref.5, f32[256,512]{1,0:T(8,128)} %fric_ref.3, ...), custom_call_target="tpu_custom_call" | custom-call | tf_op jit(solution)/shard_map/faces/pallas_call | solution.py:493
  100.6 53.8 %solve.1 = (f32[256,512]{1,0:T(8,128)}, f32[256,512]{1,0:T(8,128)}, f32[128,128]{1,0:T(8,128)}) custom-call(s32[4]{0:T(128)} %pad_add_fusion.place_ref, s32[2048]{0:T(1024)} %grow_ref.1, s32[2048]{0:T(1024)} %gcol_ref.1, s32[512]{0:T(512)} %reshape.81.block_ref, f32[256,512]{1,0:T(8,128)} %get-tuple-element.25.refs_0_.eta_ref, f32[8,256]{1,0:T(8,128)} %copy-done.5, ...), custom_call_target="tpu_custom_call" | custom-call | tf_op jit(solution)/shard_map/solve/pallas_call | solution.py:534
  154.4 9.0 %all-to-all-start.1 = ((f32[128,1,128]{2,1,0:T(1,128)}), f32[128,1,128]{2,1,0:T(1,128)S(1)}, u32[]{:S(2)}, u32[]{:S(2)}) async-start(f32[128,1,128]{2,1,0:T(1,128)} %bitcast.20), calls=%async_computation.1 | async-start | bytes 131072 | tf_op jit(solution)/shard_map/all_to_all | solution.py:565
  163.5 9.7 %all-to-all-done.1 = f32[128,1,128]{2,1,0:T(1,128)S(1)} async-done(((f32[128,1,128]{2,1,0:T(1,128)}), f32[128,1,128]{2,1,0:T(1,128)S(1)}, u32[]{:S(2)}, u32[]{:S(2)}) %all-to-all-start.1) | async-done | bytes 65568 | tf_op jit(solution)/shard_map/all_to_all | solution.py:565
  174.1 0.8 reshape.84
  (34 shorter events, 3.4 us)
Async XLA Ops:
  8.4 41.7 %all-to-all-start = ((f32[128,4224,1]{1,2,0:T(1,128)}), f32[128,4224,1]{1,2,0:T(1,128)S(1)}, u32[]{:S(2)}, u32[]{:S(2)}) async-start(f32[128,4224,1]{1,2,0:T(1,128)} %bitcast.15), calls=%async_computation | async-start | bytes 4325376 | tf_op jit(solution)/shard_map/all_to_all | solution.py:468
  22.0 42.6 %collective-permute-start.4 = (f32[24,256]{1,0:T(8,128)}, f32[24,256]{1,0:T(8,128)S(1)}, u32[]{:S(2)}, u32[]{:S(2)}) collective-permute-start(f32[24,256]{1,0:T(8,128)} %get-tuple-element.30), channel_id=1, source_target_pairs={{1,0},{2,1},{3,2},{4,3},{5,4},{6,5},{7,6},{9,8},{10,9},{11,10},{12... | collective-permute-start | bytes 73736 | tf_op jit(solution)/shard_map/ppermute | solution.py:38
  23.3 41.3 %collective-permute-start.5 = (f32[24,256]{1,0:T(8,128)}, f32[24,256]{1,0:T(8,128)S(1)}, u32[]{:S(2)}, u32[]{:S(2)}) collective-permute-start(f32[24,256]{1,0:T(8,128)} %get-tuple-element.31), channel_id=1, source_target_pairs={{0,1},{1,2},{2,3},{3,4},{4,5},{5,6},{6,7},{8,9},{9,10},{10,11},{11... | collective-permute-start | bytes 73736 | tf_op jit(solution)/shard_map/ppermute | solution.py:38
  50.1 4.0 %copy-start = (f32[128,4224,1]{1,2,0:T(1,128)}, f32[128,4224,1]{1,2,0:T(1,128)S(1)}, u32[]{:S(2)}) copy-start(f32[128,4224,1]{1,2,0:T(1,128)S(1)} %all-to-all-done) | copy-start | bytes 6488068
  59.3 15.4 %collective-permute-start = (f32[8,256]{1,0:T(8,128)}, f32[8,256]{1,0:T(8,128)S(1)}, u32[]{:S(2)}, u32[]{:S(2)}) collective-permute-start(f32[8,256]{1,0:T(8,128)} %get-tuple-element.26), channel_id=1, source_target_pairs={{1,0},{2,1},{3,2},{4,3},{5,4},{6,5},{7,6},{9,8},{10,9},{11,10},{12... | collective-permute-start | bytes 24584 | tf_op jit(solution)/shard_map/ppermute | solution.py:38
  60.6 14.2 %collective-permute-start.1 = (f32[8,256]{1,0:T(8,128)}, f32[8,256]{1,0:T(8,128)S(1)}, u32[]{:S(2)}, u32[]{:S(2)}) collective-permute-start(f32[8,256]{1,0:T(8,128)} %get-tuple-element.27), channel_id=1, source_target_pairs={{0,1},{1,2},{2,3},{3,4},{4,5},{5,6},{6,7},{8,9},{9,10},{10,11},{11... | collective-permute-start | bytes 24584 | tf_op jit(solution)/shard_map/ppermute | solution.py:38
  64.6 0.6 copy-start.1
  65.3 0.6 copy-start.2
  68.0 23.9 %collective-permute-start.6 = (f32[24,640]{1,0:T(8,128)}, f32[24,640]{1,0:T(8,128)S(1)}, u32[]{:S(2)}, u32[]{:S(2)}) collective-permute-start(f32[24,640]{1,0:T(8,128)} %get-tuple-element.32), channel_id=1, source_target_pairs={{0,8},{8,16},{16,24},{24,32},{32,40},{40,48},{48,56},{56,64},{64,7... | collective-permute-start | bytes 184328 | tf_op jit(solution)/shard_map/ppermute | solution.py:38
  72.9 19.1 %collective-permute-start.7 = (f32[24,640]{1,0:T(8,128)}, f32[24,640]{1,0:T(8,128)S(1)}, u32[]{:S(2)}, u32[]{:S(2)}) collective-permute-start(f32[24,640]{1,0:T(8,128)} %get-tuple-element.33), channel_id=1, source_target_pairs={{8,0},{16,8},{24,16},{32,24},{40,32},{48,40},{56,48},{64,56},{72,6... | collective-permute-start | bytes 184328 | tf_op jit(solution)/shard_map/ppermute | solution.py:38
  74.8 0.6 copy-start.5
  74.8 0.6 copy-start.6
  77.2 22.8 %collective-permute-start.2 = (f32[8,640]{1,0:T(8,128)}, f32[8,640]{1,0:T(8,128)S(1)}, u32[]{:S(2)}, u32[]{:S(2)}) collective-permute-start(f32[8,640]{1,0:T(8,128)} %get-tuple-element.28), channel_id=1, source_target_pairs={{0,8},{8,16},{16,24},{24,32},{32,40},{40,48},{48,56},{56,64},{64,7... | collective-permute-start | bytes 61448 | tf_op jit(solution)/shard_map/ppermute | solution.py:38
  82.3 17.7 %collective-permute-start.3 = (f32[8,640]{1,0:T(8,128)}, f32[8,640]{1,0:T(8,128)S(1)}, u32[]{:S(2)}, u32[]{:S(2)}) collective-permute-start(f32[8,640]{1,0:T(8,128)} %get-tuple-element.29), channel_id=1, source_target_pairs={{8,0},{16,8},{24,16},{32,24},{40,32},{48,40},{56,48},{64,56},{72,6... | collective-permute-start | bytes 61448 | tf_op jit(solution)/shard_map/ppermute | solution.py:38
  91.9 0.6 copy-start.3
  92.6 0.6 copy-start.4
  100.0 0.6 copy-start.7
  100.0 0.6 copy-start.8
  100.6 72.8 %copy-start.9 = (f32[16]{0:T(128)S(1)}, f32[16]{0:T(128)}, u32[]{:S(2)}) copy-start(f32[16]{0:T(128)} %slip_ref.1) | copy-start | bytes 196
  154.4 18.8 %all-to-all-start.1 = ((f32[128,1,128]{2,1,0:T(1,128)}), f32[128,1,128]{2,1,0:T(1,128)S(1)}, u32[]{:S(2)}, u32[]{:S(2)}) async-start(f32[128,1,128]{2,1,0:T(1,128)} %bitcast.20), calls=%async_computation.1 | async-start | bytes 131072 | tf_op jit(solution)/shard_map/all_to_all | solution.py:565

commit v2 on v1

--- a/solution.py
+++ b/solution.py
@@ -16,6 +16,9 @@
 CHUNK = 33
 SLOTS = 4
 LN2 = math.log(2.0)
+PUSH = -0.5 * wave_gain
+assert abs(PUSH * PUSH - speed_floor) < 1e-12
+ROUGH_SCALE = 0.5 * abs(PUSH) * 2.0 ** (7.0 / 3.0)
 F32 = jnp.float32
 I32 = jnp.int32
 
@@ -38,10 +41,39 @@
     return lax.ppermute(shard, axis, pairs)
 
 
-def pack_kernel(row_ref, slip_ref, pattern_ref, meta_ref, out_ref):
+def pack_kernel(
+    slip_ref, tile_ref, block_ref, pattern_hbm, out_ref, table_ref, pattern, row_v, row_s, sems
+):
+    load = pltpu.make_async_copy(pattern_hbm, pattern, sems.at[0])
+    load.start()
     rows = out_ref.shape[0]
-    entries = pattern_ref.shape[0]
-    per_fault = entries // slip_ref.shape[0]
+    tiles = rows // CHUNK
+    entries = tile_ref.shape[1]
+    faults = slip_ref.shape[0]
+    per_fault = entries // faults
+    tile_row = tile_ref[...]
+    tile_f = tile_row.astype(F32)
+    tile_col = jnp.broadcast_to(tile_f, (128, entries)).T
+    here = lax.broadcasted_iota(I32, (entries, 128), 0)
+    ranks = []
+    for q in range(entries // 128):
+        there = lax.broadcasted_iota(I32, (entries, 128), 1) + q * 128
+        same = (tile_col == tile_f[:, q * 128 : q * 128 + 128]) & (here < there)
+        ranks.append(jnp.sum(jnp.where(same, 1.0, 0.0), axis=0, keepdims=True))
+    rank = jnp.concatenate(ranks, axis=1).astype(I32)
+    row_v[...] = tile_row * CHUNK + rank * 8
+    place_rows = pltpu.make_async_copy(row_v, row_s, sems.at[1])
+    place_rows.start()
+    fault = lax.broadcasted_iota(I32, (1, entries), 1) // per_fault
+    slot = lax.broadcasted_iota(I32, (128, entries), 0)
+    facts = jnp.where(slot == rank, block_ref[...], 0) + jnp.where(slot == rank + 8, fault + 1, 0)
+    hot = jnp.where(lax.broadcasted_iota(I32, (tiles, entries), 0) == tile_row, 1.0, 0.0)
+    table_ref[...] = lax.dot_general(
+        hot.astype(jnp.bfloat16),
+        facts.astype(F32).astype(jnp.bfloat16),
+        (((1,), (1,)), ((), ())),
+        preferred_element_type=F32,
+    )
     zero = jnp.zeros((8, 128), F32)
 
     def clear(i, c):
@@ -49,17 +81,19 @@
         return c
 
     lax.fori_loop(0, rows // 8, clear, 0, unroll=16)
-    for t in range(rows // CHUNK):
-        out_ref[pl.ds(t * CHUNK + 32, 1), :] = meta_ref[pl.ds(t, 1), :]
+    for t in range(tiles):
+        out_ref[t * CHUNK + 32 : t * CHUNK + 33, :] = table_ref[t : t + 1, :]
+    place_rows.wait()
+    load.wait()
 
     def place(s, c):
         slip = slip_ref[s]
         for j in range(per_fault):
             i = s * per_fault + j
-            out_ref[pl.ds(row_ref[i], 8), :] = pattern_ref[i] * slip
-        return c
-
-    lax.fori_loop(0, slip_ref.shape[0], place, 0)
+            out_ref[pl.ds(row_s[0, i], 8), :] = pattern[i] * slip
+        return c
+
+    lax.fori_loop(0, faults, place, 0)
 
 
 def edges_of(first, last):
@@ -74,7 +108,12 @@
     return jnp.concatenate([east, gap, west], axis=0).T
 
 
-def scatter_kernel(block_ref, recv_ref, wet_ref, eta_ref, west_ref, east_ref, *acc):
+def scatter_kernel(
+    meta_hbm, recv_ref, wet_ref, after_a, after_b, eta_ref, west_ref, east_ref, block_ref, meta, sem, *acc
+):
+    del after_a, after_b
+    load = pltpu.make_async_copy(meta_hbm.at[:, :, pl.ds(8 * SLOTS * 128, 128)], meta, sem)
+    load.start()
     tiles = recv_ref.shape[0] // CHUNK
     rows, cols = eta_ref.shape
     across = cols // 128
@@ -86,10 +125,12 @@
         return c
 
     lax.fori_loop(0, acc[0].shape[0], clear, 0, unroll=8)
+    load.wait()
 
     def add(t, c):
         for j in range(SLOTS):
-            b = block_ref[t * SLOTS + j]
+            b = meta[t, 0, j].astype(I32)
+            block_ref[t * SLOTS + j] = b
             acc[j][b] = acc[j][b] + recv_ref[pl.ds(t * CHUNK + 8 * j, 8), :]
         return c
 
@@ -158,18 +199,18 @@
     def step(i, c):
         r = pl.multiple_of(i * 8, 8)
         n = pl.multiple_of(jnp.minimum(r + 8, rows - 8), 8)
-        for src, e_out, s_out, half in (
-            (depth_x, dde, dds, True),
-            (fric_x, rre, rrs, True),
-            (wet_out, wwe, wws, False),
+        for src, e_out, s_out, scale in (
+            (depth_x, dde, dds, 1.0),
+            (fric_x, rre, rrs, ROUGH_SCALE),
+            (wet_out, wwe, wws, None),
         ):
             here = src[pl.ds(r, 8), :]
             nxt = src[pl.ds(n, 8), :]
             east = pltpu.roll(here, cols - 1, 1)
             south = jnp.where(last, pltpu.roll(nxt, 7, 0), pltpu.roll(here, 7, 0))
-            if half:
-                e_out[pl.ds(r, 8), :] = 0.5 * (here + east)
-                s_out[pl.ds(r, 8), :] = 0.5 * (here + south)
+            if scale is not None:
+                e_out[pl.ds(r, 8), :] = scale * (here + east)
+                s_out[pl.ds(r, 8), :] = scale * (here + south)
             else:
                 e_out[pl.ds(r, 8), :] = here * east
                 s_out[pl.ds(r, 8), :] = here * south
@@ -227,26 +268,24 @@
 
 
 def face(f, s, sn, dd, rr, ww):
-    x = dd + 0.5 * (s + sn)
-    total = jnp.maximum(x, min_depth)
+    x = dd + (s + sn)
+    total = jnp.maximum(x, 2.0 * min_depth)
     diff = sn - s
-    push = (-wave_gain) * (total * diff)
+    push = total * diff
     if f is not None:
         push = push + f
-    t = push * push + speed_floor
-    rs = lax.rsqrt(t)
-    log = jnp.log(total)
-    rw = rr * jnp.exp2(log * (-7.0 / 3.0 / LN2))
-    z = rw * (t * rs)
-    inv = 1.0 / (1.0 + z)
+    t = push * push + 1.0
+    y = (rr * jnp.exp2(jnp.log(total) * (-7.0 / 3.0 / LN2))) * lax.rsqrt(t)
+    inv = 1.0 / (t * y + 1.0)
     wi = ww * inv
     flux = wi * push
-    a = wi * inv * (1.0 + speed_floor * (rw * rs))
-    depth_part = (flux * inv) * (z * jnp.exp2(log * (-1.0 / LN2))) * (7.0 / 3.0)
-    ga = wave_gain * a
-    half = jnp.where(x > min_depth, 0.5, jnp.where(x == min_depth, 0.25, 0.0))
-    u = half * (depth_part - ga * diff)
-    v = ga * total
+    a = (wi * inv) * (y + 1.0)
+    depth_part = (flux - flux * inv) * ((7.0 / 3.0) / total)
+    share = jnp.where(
+        x > 2.0 * min_depth, 1.0, jnp.where(x == 2.0 * min_depth, 0.5, 0.0)
+    )
+    u = share * (depth_part + a * diff)
+    v = a * total
     return flux, a, u + v, u - v
 
 
@@ -267,7 +306,7 @@
     wet, dde, dds, rre, rrs, wwe, wws,
     count_hbm, obs_hbm, recv_hbm,
     final_ref, adj_ref, back_ref,
-    surf, fe, fs, ae, pe, qe, as_, ps, qs, adj, ce, cs,
+    surf, fe, fs, ae, pe, qe, as_, ps, qs, adj, ce, cs, grads,
     count, obs, recv, parts, reads, sems,
 ):
     steps, rows, cols = obs.shape
@@ -285,6 +324,7 @@
     last = sub == 7
     firstrow = sub == 0
     blocks = rows // 8
+    across = own_cols // 128
 
     def nxt(i):
         return pl.multiple_of(jnp.minimum(i * 8 + 8, rows - 8), 8)
@@ -316,7 +356,7 @@
             qs[k, here, :] = q
             down = pltpu.roll(flux, 1, 0)
             div = div + (flux - jnp.where(firstrow, f_down, down))
-            surf[k + 1, here, :] = wet[here, :] * (s - mass_gain * div)
+            surf[k + 1, here, :] = wet[here, :] * (s - (mass_gain * PUSH) * div)
             return sn, sn_up, down
 
         s0 = surf[k, 0:8, :]
@@ -371,32 +411,35 @@
             bn_up = pltpu.roll(bn, 7, 0)
             b_south = jnp.where(last, bn_up, b_up)
             b_east = pltpu.roll(b, cols - 1, 1)
-            ge = mass_gain * (b_east - b)
-            gs = mass_gain * (b_south - b)
+            ge = (mass_gain * PUSH) * (b_east - b)
+            gs = (mass_gain * PUSH) * (b_south - b)
             if k < steps - 1:
                 ge = ge + ce[here, :]
                 gs = gs + cs[here, :]
             if k > 0:
                 ce[here, :] = ge * ae[k - 1, here, :]
                 cs[here, :] = gs * as_[k - 1, here, :]
-            xe = ge * qe[k, here, :]
-            xs = gs * qs[k, here, :]
+            xe = ge * pe[k, here, :]
+            xs = gs * ps[k, here, :]
             down = pltpu.roll(xs, 1, 0)
-            out = b + ge * pe[k, here, :] + pltpu.roll(xe, 1, 1)
-            out = out + gs * ps[k, here, :] + jnp.where(firstrow, x_down, down)
+            out = b + ge * qe[k, here, :] + pltpu.roll(xe, 1, 1)
+            out = out + gs * qs[k, here, :] + jnp.where(firstrow, x_down, down)
             if k > 0:
                 out = seeded(out, here, k - 1)
             adj[here, :] = out
+            if k == 0:
+                scaled = out * wet[here, :]
+                for q in range(across):
+                    grads[i * across + q] = scaled[:, q * 128 : q * 128 + 128]
             return bn, bn_up, down
 
         b0 = b_of(0)
         lax.fori_loop(
-            0, blocks, backward, (b0, pltpu.roll(b0, 7, 0), jnp.zeros((8, cols), F32))
+            0, blocks, backward, unroll=2, init_val=(b0, pltpu.roll(b0, 7, 0), jnp.zeros((8, cols), F32))
         )
 
     adj_ref[...] = adj[HALO : HALO + own_rows, 0:own_cols]
 
-    across = own_cols // 128
     tiles = recv.shape[0] // CHUNK
 
     def sens(i, c):
@@ -404,13 +447,8 @@
             products = []
             for u in range(8):
                 t = i * 8 + u
-                b = block_ref[t * SLOTS + j]
-                rb = pl.multiple_of(b // across * 8 + HALO, 8)
-                cb = pl.multiple_of(b % across * 128, 128)
-                at = (pl.ds(rb, 8), pl.ds(cb, 128))
-                products.append(
-                    (adj[at] * wet[at]) * recv[pl.ds(t * CHUNK + 8 * j, 8), :]
-                )
+                b = block_ref[t * SLOTS + j] + HALO // 8 * across
+                products.append(grads[b] * recv[pl.ds(t * CHUNK + 8 * j, 8), :])
             parts[j, pl.ds(pl.multiple_of(i * 8, 8), 8), :] = merge_rows(products)
         return c
 
@@ -447,29 +485,21 @@
     rows, cols = rows_here + 2 * HALO, cols_here + 128
     f = jax.ShapeDtypeStruct
 
-    target = foot_tile[:, 0]
-    order = jnp.arange(entries, dtype=I32)
-    earlier = (target[:, None] == target[None, :]) & (order[:, None] > order[None, :])
-    rank = jnp.sum(earlier.astype(I32), axis=1)
-    hot_tile = (jnp.arange(devices, dtype=I32)[:, None] == target[None, :]).astype(jnp.bfloat16)
-    lane = jnp.arange(128, dtype=I32)[None, :]
-    hot_slot = jnp.where(lane == rank[:, None], foot_block[:, None] + 1, 0)
-    hot_fault = jnp.where(lane == rank[:, None] + 8, order[:, None] // per_fault + 1, 0)
-    table = jnp.dot(
-        hot_tile, (hot_slot + hot_fault).astype(jnp.bfloat16), preferred_element_type=F32
-    )
-    packed = pl.pallas_call(
+    packed, table = pl.pallas_call(
         pack_kernel,
-        out_shape=f((devices * CHUNK, 128), F32),
-        in_specs=[smem(), smem(), vmem(), vmem()],
-        out_specs=vmem(),
+        out_shape=[f((devices * CHUNK, 128), F32), f((devices, 128), F32)],
+        in_specs=[smem(), vmem(), vmem(), hbm()],
+        out_specs=[vmem()] * 2,
+        scratch_shapes=[
+            pltpu.VMEM(pattern.shape, F32),
+            pltpu.VMEM((1, entries), I32),
+            pltpu.SMEM((1, entries), I32),
+            pltpu.SemaphoreType.DMA((2,)),
+        ],
         name="pack",
-    )(target * CHUNK + 8 * rank, fault_slip, pattern, table)
-    recv = lax.all_to_all(packed.reshape(-1), both, split_axis=0, concat_axis=0, tiled=True)
-    block_index = jnp.maximum(
-        recv.reshape(devices, CHUNK * 128)[:, 4096 : 4096 + SLOTS].astype(I32) - 1, 0
-    ).reshape(-1)
-    recv = recv.reshape(devices * CHUNK, 128)
+    )(fault_slip, foot_tile.reshape(1, entries), foot_block.reshape(1, entries), pattern)
+    recv_flat = lax.all_to_all(packed.reshape(-1), both, split_axis=0, concat_axis=0, tiled=True)
+    recv = recv_flat.reshape(devices * CHUNK, 128)
 
     west, east = pl.pallas_call(
         static_edge_kernel,
@@ -509,14 +539,17 @@
         name="gauges",
     )(place, gauge_row, gauge_col, observed)
 
-    eta, west, east = pl.pallas_call(
+    eta, west, east, block_index = pl.pallas_call(
         scatter_kernel,
-        out_shape=[f((rows_here, cols_here), F32)] + [f((8, rows_here), F32)] * 2,
-        in_specs=[smem(), vmem(), vmem()],
-        out_specs=[vmem()] * 3,
-        scratch_shapes=[pltpu.VMEM((rows_here * cols_here // 1024, 8, 128), F32)] * SLOTS,
+        out_shape=[f((rows_here, cols_here), F32)]
+        + [f((8, rows_here), F32)] * 2
+        + [f((devices * SLOTS,), I32)],
+        in_specs=[hbm(), vmem(), vmem(), hbm(), hbm()],
+        out_specs=[vmem()] * 3 + [smem()],
+        scratch_shapes=[pltpu.SMEM((devices, 1, 128), F32), pltpu.SemaphoreType.DMA]
+        + [pltpu.VMEM((rows_here * cols_here // 1024, 8, 128), F32)] * SLOTS,
         name="scatter",
-    )(block_index, recv, wet_mask)
+    )(recv_flat.reshape(devices, 1, CHUNK * 128), recv, wet_mask, faces[0], count)
     from_east = shifted(west, "gy", -1)
     from_west = shifted(east, "gy", 1)
     top, bottom = pl.pallas_call(
@@ -549,6 +582,7 @@
             scratch,
             scratch,
             scratch,
+            pltpu.VMEM((rows // 8 * (cols_here // 128), 8, 128), F32),
             scratch,
             pltpu.VMEM((steps, rows, cols), F32),
             pltpu.VMEM((devices * CHUNK, 128), F32),

time: 176 us -> 163 us (0.926)
  starting transfers between devices: 44.9 us -> 59.3 us
  Pallas kernels: 80.5 us -> 70.5 us
  waiting for transfers between devices: 32.5 us -> 24.5 us
  local copies, waits for them, and re-layouts: 10.2 us -> 6.07 us
  other arithmetic: 4.86 us -> 1.38 us
    all_to_all x1, waiting for transfers between devices: 22.8 us -> 0.01 us  [body(): lax.all_to_all(packed.reshape(-1), both, split_axis=0, concat_axis=0, til...]
    ppermute x8, waiting for transfers between devices: 0.02 us -> 14.8 us  [shifted(): return lax.ppermute(shard, axis, pairs)]
    pallas_call x1, Pallas kernels: 53.8 us -> 40.9 us  [body(): pl.pallas_call(solve_kernel, out_shape=[tile, tile, f((devices, 128), F32...]
    ppermute x8, starting transfers between devices: 24.4 us -> 34 us  [shifted(): return lax.ppermute(shard, axis, pairs)]
    all_to_all x1, starting transfers between devices: 9.03 us -> 13.8 us  [body(): lax.all_to_all(back, both, split_axis=0, concat_axis=0, tiled=True)]
    all_to_all x1 -> x0, local copies, waits for them, and re-layouts: 4.03 us -> none  [body(): lax.all_to_all(packed.reshape(-1), both, split_axis=0, concat_axis=0, til...]
    pallas_call x1, Pallas kernels: 3.68 us -> 6.15 us  [body(): pl.pallas_call(scatter_kernel, out_shape=[f((rows_here, cols_here), F32)]...]
    add x2 -> x0, other arithmetic: 1.93 us -> none  [the longest x1 1.25 us: body(): rank[:, None] + 8]
  transfers between devices with their start and end apart: 10 -> 10, of which waited for: 2 -> 4; matrix products, arithmetic and copies ran while one was open for 4% -> 0% of each run, Pallas kernels for 13% -> 11%
where the time goes in v2:
time: 163 us
  Pallas kernels  70.5 us (43%)
  starting transfers between devices  59.3 us (36%)
  waiting for transfers between devices  24.5 us (15%)
  local copies, waits for them, and re-layouts  6.07 us (4%)
    pallas_call x1, Pallas kernels, body(): pl.pallas_call(solve_kernel, out_shape=[tile, tile, f((devices, 128), F32...  40.9 us
    ppermute x8, starting transfers between devices, shifted(): return lax.ppermute(shard, axis, pairs)  34 us
    ppermute x8, waiting for transfers between devices, shifted(): return lax.ppermute(shard, axis, pairs)  14.8 us
    all_to_all x1, starting transfers between devices, body(): lax.all_to_all(back, both, split_axis=0, concat_axis=0, tiled=True)  13.8 us
    all_to_all x1, starting transfers between devices, body(): lax.all_to_all(packed.reshape(-1), both, split_axis=0, concat_axis=0, til...  11.5 us
    all_to_all x1, waiting for transfers between devices, body(): lax.all_to_all(back, both, split_axis=0, concat_axis=0, tiled=True)  9.73 us
    pallas_call x1, Pallas kernels, body(): pl.pallas_call(gauge_kernel, out_shape=[grid, f((steps, rows, cols), F32)...  7.03 us
    pallas_call x1, Pallas kernels, body(): pl.pallas_call(face_static_kernel, out_shape=[grid] * 7, in_specs=[vmem()...  6.8 us
  transfers between devices with their start and end apart: 10, of which 4 were waited for; matrix products, arithmetic and copies ran while one was open for 0% of the time, Pallas kernels for 11%

profile of v2, /device:TPU:1, one launch (start us, length us, event | category | flops | bytes accessed | tf_op | source)
XLA Modules:
  0.0 162.5 jit_solution(12630593505675801827)
XLA Ops:
  0.6 3.6 %pack.1 = (f32[4224,128]{1,0:T(8,128)}, f32[128,128]{1,0:T(8,128)}) custom-call(f32[16]{0:T(128)} %slip_ref.1, s32[1,256]{1,0:T(1,128)} %bitcast.22, s32[1,256]{1,0:T(1,128)} %bitcast.23, f32[256,8,128]{2,1,0:T(8,128)} %pattern_hbm.1), custom_call_target="tpu_custom_call" | custom-call | tf_op jit(solution)/shard_map/pack/pallas_call | solution.py:488
  4.2 11.5 %all-to-all-start = ((f32[128,4224,1]{1,2,0:T(1,128)}), f32[128,4224,1]{1,2,0:T(1,128)S(1)}, u32[]{:S(2)}, u32[]{:S(2)}) async-start(f32[128,4224,1]{1,2,0:T(1,128)} %bitcast.17), calls=%async_computation | async-start | bytes 4325376 | tf_op jit(solution)/shard_map/all_to_all | solution.py:501
  15.7 2.1 %static_edges.1 = (f32[24,256]{1,0:T(8,128)}, f32[24,256]{1,0:T(8,128)}) custom-call(f32[256,512]{1,0:T(8,128)} %depth_ref.3, s32[256,512]{1,0:T(8,128)} %wet_ref.5, f32[256,512]{1,0:T(8,128)} %fric_ref.3), custom_call_target="tpu_custom_call" | custom-call | tf_op jit(solution)/shard_map/static_edges/pallas_call | solution.py:504
  17.9 1.3 collective-permute-start
  19.2 4.0 %collective-permute-start.1 = (f32[24,256]{1,0:T(8,128)}, f32[24,256]{1,0:T(8,128)S(1)}, u32[]{:S(2)}, u32[]{:S(2)}) collective-permute-start(f32[24,256]{1,0:T(8,128)} %get-tuple-element.30), channel_id=1, source_target_pairs={{0,1},{1,2},{2,3},{3,4},{4,5},{5,6},{6,7},{8,9},{9,10},{10,11},{11... | collective-permute-start | bytes 73736 | tf_op jit(solution)/shard_map/ppermute | solution.py:41
  23.2 8.9 %collective-permute-done.refs_3_.east_ref = f32[24,256]{1,0:T(8,128)S(1)} collective-permute-done((f32[24,256]{1,0:T(8,128)}, f32[24,256]{1,0:T(8,128)S(1)}, u32[]{:S(2)}, u32[]{:S(2)}) %collective-permute-start) | collective-permute-done | bytes 24608 | tf_op jit(solution)/shard_map/ppermute | solution.py:41
  32.1 0.6 copy-done.1
  32.7 0.6 copy-done.2
  33.3 2.2 %static_rims.1 = (f32[24,640]{1,0:T(8,128)}, f32[24,640]{1,0:T(8,128)}) custom-call(f32[256,512]{1,0:T(8,128)} %depth_ref.3, s32[256,512]{1,0:T(8,128)} %wet_ref.5, f32[256,512]{1,0:T(8,128)} %fric_ref.3, f32[24,256]{1,0:T(8,128)} %copy-done.1, f32[24,256]{1,0:T(8,128)} %copy-done.2), custom_call_target="tpu_custom_call" | custom-call | tf_op jit(solution)/shard_map/static_rims/pallas_call | solution.py:513
  35.5 1.9 %collective-permute-start.2 = (f32[24,640]{1,0:T(8,128)}, f32[24,640]{1,0:T(8,128)S(1)}, u32[]{:S(2)}, u32[]{:S(2)}) collective-permute-start(f32[24,640]{1,0:T(8,128)} %get-tuple-element.31), channel_id=1, source_target_pairs={{0,8},{8,16},{16,24},{24,32},{32,40},{40,48},{48,56},{56,64},{64,7... | collective-permute-start | bytes 184328 | tf_op jit(solution)/shard_map/ppermute | solution.py:41
  37.4 6.5 %collective-permute-start.3 = (f32[24,640]{1,0:T(8,128)}, f32[24,640]{1,0:T(8,128)S(1)}, u32[]{:S(2)}, u32[]{:S(2)}) collective-permute-start(f32[24,640]{1,0:T(8,128)} %get-tuple-element.32), channel_id=1, source_target_pairs={{8,0},{16,8},{24,16},{32,24},{40,32},{48,40},{56,48},{64,56},{72,6... | collective-permute-start | bytes 184328 | tf_op jit(solution)/shard_map/ppermute | solution.py:41
  43.9 0.7 pad_add_fusion.place_ref
  44.6 7.0 %gauges.1 = (f32[272,640]{1,0:T(8,128)}, f32[4,272,640]{2,1,0:T(8,128)}) custom-call(s32[4]{0:T(128)} %pad_add_fusion.place_ref, s32[2048]{0:T(1024)} %grow_ref.1, s32[2048]{0:T(1024)} %gcol_ref.1, f32[4,2048]{1,0:T(4,128)} %obs_ref.1), custom_call_target="tpu_custom_call" | custom-call | tf_op jit(solution)/shard_map/gauges/pallas_call | solution.py:534
  51.6 0.6 copy-done.4
  52.2 0.6 copy-done.5
  52.9 6.8 %faces.1 = (f32[272,640]{1,0:T(8,128)}, f32[272,640]{1,0:T(8,128)}, f32[272,640]{1,0:T(8,128)}, f32[272,640]{1,0:T(8,128)}, f32[272,640]{1,0:T(8,128)}, /*index=5*/f32[272,640]{1,0:T(8,128)}, f32[272,640]{1,0:T(8,128)}) custom-call(f32[256,512]{1,0:T(8,128)} %depth_ref.3, s32[256,512]{1,0:T(8,128)} %wet_ref.5, f32[256,512]{1,0:T(8,128)} %fric_ref.3, ...), custom_call_target="tpu_custom_call" | custom-call | tf_op jit(solution)/shard_map/faces/pallas_call | solution.py:523
  59.7 1.4 copy-done
  61.0 6.2 %scatter.1 = (f32[256,512]{1,0:T(8,128)}, f32[8,256]{1,0:T(8,128)}, f32[8,256]{1,0:T(8,128)}, s32[512]{0:T(512)}) custom-call(f32[128,1,4224]{2,1,0:T(1,128)} %bitcast.14, f32[4224,128]{1,0:T(8,128)} %bitcast.15, s32[256,512]{1,0:T(8,128)} %wet_ref.5, f32[272,640]{1,0:T(8,128)} %get-tuple-element.33.after_a.wet, f32[272,640]{1,0:T(8,128)} %get-tuple-element.34.after_b.count_hbm), custom_call_target="tpu_custom_call" | custom-call | tf_op jit(solution)/shard_map/scatter/pallas_call | solution.py:542
  67.2 1.3 collective-permute-start.4
  68.5 11.1 %collective-permute-start.5 = (f32[8,256]{1,0:T(8,128)}, f32[8,256]{1,0:T(8,128)S(1)}, u32[]{:S(2)}, u32[]{:S(2)}) collective-permute-start(f32[8,256]{1,0:T(8,128)} %get-tuple-element.38), channel_id=1, source_target_pairs={{0,1},{1,2},{2,3},{3,4},{4,5},{5,6},{6,7},{8,9},{9,10},{10,11},{11... | collective-permute-start | bytes 24584 | tf_op jit(solution)/shard_map/ppermute | solution.py:41
  79.6 1.0 collective-permute-done.5.refs_2_.west_ref
  80.6 0.6 copy-done.7
  81.2 1.8 %eta_rims.1 = (f32[8,640]{1,0:T(8,128)}, f32[8,640]{1,0:T(8,128)}) custom-call(f32[256,512]{1,0:T(8,128)} %get-tuple-element.36.refs_0_.eta_ref, f32[8,256]{1,0:T(8,128)} %copy-done.6, f32[8,256]{1,0:T(8,128)} %copy-done.7), custom_call_target="tpu_custom_call" | custom-call | tf_op jit(solution)/shard_map/eta_rims/pallas_call | solution.py:555
  83.0 6.0 %collective-permute-start.6 = (f32[8,640]{1,0:T(8,128)}, f32[8,640]{1,0:T(8,128)S(1)}, u32[]{:S(2)}, u32[]{:S(2)}) collective-permute-start(f32[8,640]{1,0:T(8,128)} %get-tuple-element.39), channel_id=1, source_target_pairs={{0,8},{8,16},{16,24},{24,32},{32,40},{40,48},{48,56},{56,64},{64,7... | collective-permute-start | bytes 61448 | tf_op jit(solution)/shard_map/ppermute | solution.py:41
  88.9 1.9 %collective-permute-start.7 = (f32[8,640]{1,0:T(8,128)}, f32[8,640]{1,0:T(8,128)S(1)}, u32[]{:S(2)}, u32[]{:S(2)}) collective-permute-start(f32[8,640]{1,0:T(8,128)} %get-tuple-element.40), channel_id=1, source_target_pairs={{8,0},{16,8},{24,16},{32,24},{40,32},{48,40},{56,48},{64,56},{72,6... | collective-permute-start | bytes 61448 | tf_op jit(solution)/shard_map/ppermute | solution.py:41
  90.9 4.9 %collective-permute-done.7.south_ref = f32[8,640]{1,0:T(8,128)S(1)} collective-permute-done((f32[8,640]{1,0:T(8,128)}, f32[8,640]{1,0:T(8,128)S(1)}, u32[]{:S(2)}, u32[]{:S(2)}) %collective-permute-start.7) | collective-permute-done | bytes 20512 | tf_op jit(solution)/shard_map/ppermute | solution.py:41
  95.8 0.6 copy-done.9
  96.4 40.9 %solve.1 = (f32[256,512]{1,0:T(8,128)}, f32[256,512]{1,0:T(8,128)}, f32[128,128]{1,0:T(8,128)}) custom-call(s32[4]{0:T(128)} %pad_add_fusion.place_ref, s32[2048]{0:T(1024)} %grow_ref.1, s32[2048]{0:T(1024)} %gcol_ref.1, s32[512]{0:T(512)} %get-tuple-element.35.block_ref, f32[256,512]{1,0:T(8,128)} %get-tuple-element.36.refs_0_.eta_ref, f32[8,256]{1,0:T(8,128)} %copy-done.6, ...), custom_call_target="tpu_custom_call" | custom-call | tf_op jit(solution)/shard_map/solve/pallas_call | solution.py:567
  137.2 13.8 %all-to-all-start.1 = ((f32[128,1,128]{2,1,0:T(1,128)}), f32[128,1,128]{2,1,0:T(1,128)S(1)}, u32[]{:S(2)}, u32[]{:S(2)}) async-start(f32[128,1,128]{2,1,0:T(1,128)} %bitcast.21), calls=%async_computation.1 | async-start | bytes 131072 | tf_op jit(solution)/shard_map/all_to_all | solution.py:599
  151.1 9.7 %all-to-all-done.1 = f32[128,1,128]{2,1,0:T(1,128)S(1)} async-done(((f32[128,1,128]{2,1,0:T(1,128)}), f32[128,1,128]{2,1,0:T(1,128)S(1)}, u32[]{:S(2)}, u32[]{:S(2)}) %all-to-all-start.1) | async-done | bytes 65568 | tf_op jit(solution)/shard_map/all_to_all | solution.py:599
  161.1 0.5 div.3
  161.8 0.8 reshape.41
  (28 shorter events, 0.5 us)
Async XLA Ops:
  4.2 55.4 %all-to-all-start = ((f32[128,4224,1]{1,2,0:T(1,128)}), f32[128,4224,1]{1,2,0:T(1,128)S(1)}, u32[]{:S(2)}, u32[]{:S(2)}) async-start(f32[128,4224,1]{1,2,0:T(1,128)} %bitcast.17), calls=%async_computation | async-start | bytes 4325376 | tf_op jit(solution)/shard_map/all_to_all | solution.py:501
  17.9 14.2 %collective-permute-start = (f32[24,256]{1,0:T(8,128)}, f32[24,256]{1,0:T(8,128)S(1)}, u32[]{:S(2)}, u32[]{:S(2)}) collective-permute-start(f32[24,256]{1,0:T(8,128)} %get-tuple-element.29), channel_id=1, source_target_pairs={{1,0},{2,1},{3,2},{4,3},{5,4},{6,5},{7,6},{9,8},{10,9},{11,10},{12... | collective-permute-start | bytes 73736 | tf_op jit(solution)/shard_map/ppermute | solution.py:41
  19.2 12.9 %collective-permute-start.1 = (f32[24,256]{1,0:T(8,128)}, f32[24,256]{1,0:T(8,128)S(1)}, u32[]{:S(2)}, u32[]{:S(2)}) collective-permute-start(f32[24,256]{1,0:T(8,128)} %get-tuple-element.30), channel_id=1, source_target_pairs={{0,1},{1,2},{2,3},{3,4},{4,5},{5,6},{6,7},{8,9},{9,10},{10,11},{11... | collective-permute-start | bytes 73736 | tf_op jit(solution)/shard_map/ppermute | solution.py:41
  32.1 0.6 copy-start.1
  32.7 0.6 copy-start.2
  35.5 16.1 %collective-permute-start.2 = (f32[24,640]{1,0:T(8,128)}, f32[24,640]{1,0:T(8,128)S(1)}, u32[]{:S(2)}, u32[]{:S(2)}) collective-permute-start(f32[24,640]{1,0:T(8,128)} %get-tuple-element.31), channel_id=1, source_target_pairs={{0,8},{8,16},{16,24},{24,32},{32,40},{40,48},{48,56},{56,64},{64,7... | collective-permute-start | bytes 184328 | tf_op jit(solution)/shard_map/ppermute | solution.py:41
  37.4 14.2 %collective-permute-start.3 = (f32[24,640]{1,0:T(8,128)}, f32[24,640]{1,0:T(8,128)S(1)}, u32[]{:S(2)}, u32[]{:S(2)}) collective-permute-start(f32[24,640]{1,0:T(8,128)} %get-tuple-element.32), channel_id=1, source_target_pairs={{8,0},{16,8},{24,16},{32,24},{40,32},{48,40},{56,48},{64,56},{72,6... | collective-permute-start | bytes 184328 | tf_op jit(solution)/shard_map/ppermute | solution.py:41
  51.6 0.6 copy-start.4
  52.2 0.6 copy-start.5
  59.7 1.4 copy-start
  67.2 12.4 %collective-permute-start.4 = (f32[8,256]{1,0:T(8,128)}, f32[8,256]{1,0:T(8,128)S(1)}, u32[]{:S(2)}, u32[]{:S(2)}) collective-permute-start(f32[8,256]{1,0:T(8,128)} %get-tuple-element.37), channel_id=1, source_target_pairs={{1,0},{2,1},{3,2},{4,3},{5,4},{6,5},{7,6},{9,8},{10,9},{11,10},{12... | collective-permute-start | bytes 24584 | tf_op jit(solution)/shard_map/ppermute | solution.py:41
  68.5 12.1 %collective-permute-start.5 = (f32[8,256]{1,0:T(8,128)}, f32[8,256]{1,0:T(8,128)S(1)}, u32[]{:S(2)}, u32[]{:S(2)}) collective-permute-start(f32[8,256]{1,0:T(8,128)} %get-tuple-element.38), channel_id=1, source_target_pairs={{0,1},{1,2},{2,3},{3,4},{4,5},{5,6},{6,7},{8,9},{9,10},{10,11},{11... | collective-permute-start | bytes 24584 | tf_op jit(solution)/shard_map/ppermute | solution.py:41
  79.6 1.0 copy-start.6
  80.6 0.6 copy-start.7
  83.0 7.9 %collective-permute-start.6 = (f32[8,640]{1,0:T(8,128)}, f32[8,640]{1,0:T(8,128)S(1)}, u32[]{:S(2)}, u32[]{:S(2)}) collective-permute-start(f32[8,640]{1,0:T(8,128)} %get-tuple-element.39), channel_id=1, source_target_pairs={{0,8},{8,16},{16,24},{24,32},{32,40},{40,48},{48,56},{56,64},{64,7... | collective-permute-start | bytes 61448 | tf_op jit(solution)/shard_map/ppermute | solution.py:41
  88.9 6.8 %collective-permute-start.7 = (f32[8,640]{1,0:T(8,128)}, f32[8,640]{1,0:T(8,128)S(1)}, u32[]{:S(2)}, u32[]{:S(2)}) collective-permute-start(f32[8,640]{1,0:T(8,128)} %get-tuple-element.40), channel_id=1, source_target_pairs={{8,0},{16,8},{24,16},{32,24},{40,32},{48,40},{56,48},{64,56},{72,6... | collective-permute-start | bytes 61448 | tf_op jit(solution)/shard_map/ppermute | solution.py:41
  90.9 4.9 %copy-start.8 = (f32[8,640]{1,0:T(8,128)}, f32[8,640]{1,0:T(8,128)S(1)}, u32[]{:S(2)}) copy-start(f32[8,640]{1,0:T(8,128)S(1)} %collective-permute-done.6.north_ref) | copy-start | bytes 61444
  95.7 0.6 copy-start.9
  96.4 54.6 %copy-start.3 = (f32[128,128]{1,0:T(8,128)S(1)}, f32[128,128]{1,0:T(8,128)}, u32[]{:S(2)}) copy-start(f32[128,128]{1,0:T(8,128)} %get-tuple-element.51) | copy-start | bytes 196612
  96.4 64.8 %copy-start.10 = (f32[16]{0:T(128)S(1)}, f32[16]{0:T(128)}, u32[]{:S(2)}) copy-start(f32[16]{0:T(128)} %slip_ref.1) | copy-start | bytes 196
  137.2 23.7 %all-to-all-start.1 = ((f32[128,1,128]{2,1,0:T(1,128)}), f32[128,1,128]{2,1,0:T(1,128)S(1)}, u32[]{:S(2)}, u32[]{:S(2)}) async-start(f32[128,1,128]{2,1,0:T(1,128)} %bitcast.21), calls=%async_computation.1 | async-start | bytes 131072 | tf_op jit(solution)/shard_map/all_to_all | solution.py:599
